TPU v7x, 512 devices: a whole 4x8x8 slice. The times are simulated.
512 devices in a mesh: row: 32 (over z, y_lo, core), col: 16 (over y_hi, x).
Axes of the slice: x: 4, y: 8 (y_hi: 4, y_lo: 2; y = y_hi * 2 + y_lo), z: 8, core: 2. Of those that a mesh axis runs over, the one named last changes fastest.
Arguments:
- r_vals: bfloat16 [65536, 2048], P('row', 'col'), may hold values from -6 to 6
- s_vals: bfloat16 [2048, 4096], P('row', 'col'), may hold values from -0.125 to 0.125
- t_vals: bfloat16 [4096, 65536], P(None, ('row', 'col')), may hold values from -6 to 6
- r_pattern: int32 [512, 16], replicated, may hold values 0 or 1
- s_pattern: int32 [16, 32], replicated, may hold values 0 or 1
- t_pattern: int32 [32, 512], replicated, may hold values 0 or 1
Outputs:
- joined: bfloat16 [65536, 4096], P('row', 'col')
All inputs are finite; a program needn't handle non-finite values.
Results may differ from a plain program's by a relative error of at most 0.001.
Values may be sent and summed in bfloat16 or wider, within the bound.
A program may use at most 64 MiB of HBM per device.

v0:
```python
import jax
import jax.numpy as jnp
from jax import lax
from jax.sharding import PartitionSpec as P

BLK = 128


def sent_to_all(value, axis):
    peers = lax.axis_size(axis)
    return lax.all_to_all(
        jnp.broadcast_to(value[None], (peers, *value.shape)), axis, 0, 0, tiled=True
    )


def in_order(blocks, dim):
    blocks = jnp.moveaxis(blocks, 0, dim)
    dims = blocks.shape
    return blocks.reshape(*dims[:dim], dims[dim] * dims[dim + 1], *dims[dim + 2 :])


def gather_directly(value, axis, dim):
    blocks = sent_to_all(value, axis)
    return in_order(blocks, dim)


def body(r_vals, s_vals, t_vals, r_pattern, s_pattern, t_pattern):
    row_index = lax.axis_index("row")
    col_index = lax.axis_index("col")
    a_rows = r_vals.shape[0]
    c_cols = s_vals.shape[1]
    a_tiles = a_rows // BLK
    c_tiles = c_cols // BLK
    r_rows = lax.dynamic_slice_in_dim(r_pattern, row_index * a_tiles, a_tiles, 0).astype(
        jnp.bfloat16
    )
    s_cols = lax.dynamic_slice_in_dim(s_pattern, col_index * c_tiles, c_tiles, 1).astype(
        jnp.bfloat16
    )
    r_all = lax.all_gather(r_vals, "col", axis=1, tiled=True)
    s_all = gather_directly(s_vals, "row", 0)
    r_mask = jnp.repeat(jnp.repeat(r_rows, BLK, axis=0), BLK, axis=1)
    s_mask = jnp.repeat(jnp.repeat(s_cols, BLK, axis=0), BLK, axis=1)
    paths = jnp.dot(r_all * r_mask, s_all * s_mask, preferred_element_type=jnp.float32)
    t_tiles = lax.dynamic_slice_in_dim(t_pattern, col_index * c_tiles, c_tiles, 0)
    t_tiles = lax.dynamic_slice_in_dim(t_tiles, row_index * a_tiles, a_tiles, 1).astype(
        jnp.bfloat16
    )
    t_block = lax.all_to_all(t_vals, "col", split_axis=0, concat_axis=1, tiled=True)
    t_mask = jnp.repeat(jnp.repeat(t_tiles, BLK, axis=0), BLK, axis=1)
    mirror = (t_block * t_mask).T
    return (paths * mirror.astype(jnp.float32)).astype(jnp.bfloat16)


def solution(mesh):
    placed = (P("row", "col"), P("row", "col"), P(None, ("row", "col")), P(), P(), P())
    return jax.shard_map(
        body, mesh=mesh, in_specs=placed, out_specs=P("row", "col"), check_vma=False
    )
```

profile of v0, /device:TPU:1, one launch (start us, length us, event | category | flops | bytes accessed | tf_op | source)
XLA Modules:
  0.0 184.2 jit_solution(13213994456814922172)
XLA Ops:
  6.5 0.0 all-gather.2.cloned.1.call-start
  6.5 0.7 all-gather.2.cloned.1.call-update
  7.3 1.5 copy.8
  8.7 43.5 %all_to_all.21 = bf16[16,256,128]{1,2,0:T(8,128)(2,1)S(1)} all-to-all(bf16[16,256,128]{1,2,0:T(8,128)(2,1)S(1)} %copy.8), channel_id=1, replica_groups=mesh['row'=32,'col'=16] {'col'}, dimensions={0} | all-to-all | bytes 2097152 | tf_op jit(solution)/shard_map/all_to_all | solution.py:49
  52.3 1.8 %broadcast_in_dim.26 = bf16[32,64,256]{2,1,0:T(8,128)(2,1)} broadcast(bf16[64,256]{1,0:T(8,128)(2,1)} %param.7), dimensions={1,2} | broadcast | bytes 1081344 | tf_op jit(solution)/shard_map/broadcast_in_dim | solution.py:12
  54.1 15.4 %all-to-all-start = ((bf16[32,64,256]{2,1,0:T(8,128)(2,1)}), bf16[32,64,256]{2,1,0:T(8,128)(2,1)S(1)}, u32[]{:S(2)}, u32[]{:S(2)}) async-start(bf16[32,64,256]{2,1,0:T(8,128)(2,1)} %broadcast_in_dim.26), calls=%async_computation | async-start | bytes 2097152 | tf_op jit(solution)/shard_map/all_to_all | solution.py:11
  69.5 0.8 dynamic-slice_convert_fusion.1
  70.3 0.1 copy.7
  70.4 0.8 dynamic-slice_convert_fusion.2
  71.2 0.1 copy.9
  71.3 0.1 broadcast_in_dim.29
  71.4 0.8 dynamic-slice_convert_fusion
  72.2 0.1 bitcast_multiply_fusion.8
  72.3 25.5 %all-to-all-done = bf16[32,64,256]{2,1,0:T(8,128)(2,1)S(1)} async-done(((bf16[32,64,256]{2,1,0:T(8,128)(2,1)}), bf16[32,64,256]{2,1,0:T(8,128)(2,1)S(1)}, u32[]{:S(2)}, u32[]{:S(2)}) %all-to-all-start) | async-done | bytes 1048608 | tf_op jit(solution)/shard_map/all_to_all | solution.py:11
  97.8 60.9 %all-gather.2.cloned.1.call-done = bf16[2048,2048]{1,0:T(8,128)(2,1)} async-done(((bf16[2048,128]{1,0:T(8,128)(2,1)}), bf16[2048,2048]{1,0:T(8,128)(2,1)}) %all-gather.2.cloned.1.call-update) | async-done | bytes 8388624 | tf_op jit(solution)/shard_map/all_gather | solution.py:40
  158.7 0.0 copy-start
  158.7 0.1 broadcast_in_dim.27
  158.8 5.8 %broadcast_in_dim.28 = bf16[2048,2,128]{2,1,0:T(2,128)(2,1)S(1)} broadcast(bf16[2048,2]{1,0:T(8,128)(2,1)S(1)} %bitcast.31), dimensions={0,1} | broadcast | bytes 1056768 | tf_op jit(solution)/shard_map/broadcast_in_dim | solution.py:43
  164.5 0.1 broadcast_in_dim.24
  164.6 9.0 %broadcast_in_dim.25 = bf16[2048,16,128]{2,1,0:T(8,128)(2,1)S(1)} broadcast(bf16[2048,16]{1,0:T(8,128)(2,1)S(1)} %bitcast.32), dimensions={0,1} | broadcast | bytes 8454144 | tf_op jit(solution)/shard_map/broadcast_in_dim | solution.py:42
  173.6 0.0 copy-done
  173.6 3.8 %fusion.3 = bf16[2048,256]{1,0:T(8,128)(2,1)} fusion(bf16[2048,2048]{1,0:T(8,128)(2,1)S(1)} %copy-done, bf16[256,8,16,128]{3,2,1,0:T(8,128)(2,1)S(1)} %bitcast.30, bf16[256,2048]{0,1:T(8,128)(2,1)S(1)} %bitcast.36, bf16[2048,256]{1,0:T(8,128)(2,1)S(1)} %bitcast.35, bf16[256,8,2,128]{3,2,1,0:T(2,128)(2,1)S(1)} %bitcast.33), kind=kOutput, calls=%fused_computation.4 | convolution fusion | flops 2153775104 | bytes 20971520 | tf_op jit(solution)/shard_map/dot_general | solution.py:44
  (1 shorter events, 0.0 us)
Async XLA Ops:
  6.5 152.1 %all-gather.2.cloned.1.call-start = ((), (), s32[]{:S(2)}) async-start(), calls=%async_computation.2 | async-start | bytes 8912896 | tf_op jit(solution)/shard_map/all_gather | solution.py:40
  54.1 43.6 %all-to-all-start = ((bf16[32,64,256]{2,1,0:T(8,128)(2,1)}), bf16[32,64,256]{2,1,0:T(8,128)(2,1)S(1)}, u32[]{:S(2)}, u32[]{:S(2)}) async-start(bf16[32,64,256]{2,1,0:T(8,128)(2,1)} %broadcast_in_dim.26), calls=%async_computation | async-start | bytes 2097152 | tf_op jit(solution)/shard_map/all_to_all | solution.py:11
  158.7 14.9 %copy-start = (bf16[2048,2048]{1,0:T(8,128)(2,1)S(1)}, bf16[2048,2048]{1,0:T(8,128)(2,1)}, u32[]{:S(2)}) copy-start(bf16[2048,2048]{1,0:T(8,128)(2,1)} %all-gather.2.cloned.1.call-done) | copy-start | bytes 25165828
Sparse Core Ops, SparseCore 0:
  10.3 148.3 all-gather.1
where the time goes:
time: 185 us; the launch traced here: 184 us
  waiting for transfers between devices  87.1 us (47%)
  blocking collectives  43.5 us (24%)
  local copies, waits for them, and re-layouts  18.5 us (10%)
  starting transfers between devices  15.4 us (8%)
  between operations  13.5 us (7%)
  matrix products  3.8 us (2%)
  other arithmetic  2.43 us (1%)
    all_gather x1, waiting for transfers between devices, body(): r_all = lax.all_gather(r_vals, 'col', axis=1, tiled=True)  60.9 us
    all_to_all x1, blocking collectives, body(): lax.all_to_all(t_vals, 'col', split_axis=0, concat_axis=1, tiled=True)  43.5 us
    all_to_all x1, waiting for transfers between devices, sent_to_all(): lax.all_to_all(jnp.broadcast_to(value[None], (peers, *value.shape)), axis...  25.5 us
    all_to_all x1, starting transfers between devices, sent_to_all(): lax.all_to_all(jnp.broadcast_to(value[None], (peers, *value.shape)), axis...  15.4 us
    broadcast_in_dim x2, local copies, waits for them, and re-layouts, body(): r_mask = jnp.repeat(jnp.repeat(r_rows, BLK, axis=0), BLK, axis=1)  9.03 us
    broadcast_in_dim x2, local copies, waits for them, and re-layouts, body(): s_mask = jnp.repeat(jnp.repeat(s_cols, BLK, axis=0), BLK, axis=1)  5.85 us
    dot_general x1, matrix products, body(): jnp.dot(r_all * r_mask, s_all * s_mask, preferred_element_type=jnp.float32)  3.8 us
  transfers between devices with their start and end apart: 2, of which 2 were waited for; matrix products, arithmetic and copies ran while one was open for 3% of the time, Pallas kernels for 0%

commit v1 on v0

v1 whole, which is shorter than its diff:
```python
import jax
import jax.numpy as jnp
from jax import lax
from jax.experimental import pallas as pl
from jax.experimental.pallas import tpu as pltpu
from jax.sharding import PartitionSpec as P

MESH = pl.DeviceIdType.MESH
BLK = 128
PASSES = 2
H = 512 // PASSES
SEMS = 144


def kernel(
    r_ref, s_ref, t_ref, rp_ref, sp_ref, tp_ref, out_ref,
    rbuf, rrel, sbuf, tbuf, trel, obuf, orel, reff, seff, rp, sp, tp, ssem, rsem, lsem,
):
    row, col = lax.axis_index("row"), lax.axis_index("col")
    z, yl, core = lax.div(row, 4), lax.rem(lax.div(row, 2), 2), lax.rem(row, 2)
    yh, x = lax.div(col, 4), lax.rem(col, 4)
    xs = [lax.rem(x + d, 4) for d in range(4)]
    ys = [lax.rem(yh + d, 4) for d in range(4)]
    zs = [lax.rem(z + d, 8) for d in range(8)]
    low = yl * 2 + core
    x_to = [(row, yh * 4 + xs[1]), (row, yh * 4 + xs[3])]
    y_to = [(row, ys[1] * 4 + x), (row, ys[3] * 4 + x)]
    z_to = [(zs[1] * 4 + low, col), (zs[7] * 4 + low, col)]
    pair = (z * 4 + (1 - yl) * 2 + core, col)
    twin = (row + 1 - 2 * core, col)
    par = lax.rem(yh, 2)
    pars = [1 - par, par]
    block = [yh, ys[1], ys[3], ys[2]]
    half = [pl.ds(0, H // 2), pl.ds(H // 2, H // 2)]

    sent = {}

    def send(name, src, dst, device):
        n = len(sent)
        sent[name] = pltpu.make_async_remote_copy(
            src_ref=src, dst_ref=dst, send_sem=ssem.at[n], recv_sem=rsem.at[n],
            device_id=device, device_id_type=MESH,
        )
        sent[name].start()

    def arrive(*name):
        sent[name].wait_recv()

    local = []

    def fetch(src, dst):
        local.append(pltpu.make_async_copy(src, dst, lsem.at[len(local)]))
        local[-1].start()
        return local[-1]

    barrier = pltpu.get_barrier_semaphore()
    for device in (*x_to, *y_to, *z_to, pair, twin):
        pl.semaphore_signal(barrier, inc=1, device_id=device, device_id_type=MESH)
    own_s = fetch(s_ref, sbuf.at[yh, core, z, yl])
    own_r = [fetch(r_ref.at[yh, p], rbuf.at[col, p]) for p in range(PASSES)]
    own_t = [fetch(t_ref.at[:, pars[ph], x], tbuf.at[ph, x]) for ph in range(2)]
    masks = [
        fetch(rp_ref.at[pl.ds(pl.multiple_of(row * 16, 16), 16)], rp),
        fetch(sp_ref, sp),
        fetch(tp_ref.at[:, pl.ds(pl.multiple_of(lax.div(row, 8) * 128, 128), 128)], tp),
    ]
    pl.semaphore_wait(barrier, 8)

    def r_legs(p):
        for d in range(2):
            send(("RL1", p, d), r_ref.at[ys[2], p, half[d]], rrel.at[p, d], y_to[d])

    def r_direct(p):
        for d in range(2):
            send(("RY", p, d), r_ref.at[ys[(1, 3)[d]], p], rbuf.at[col, p], y_to[d])

    def r_relay(p):
        for d in range(2):
            arrive("RL1", p, d)
            origin = ys[(3, 1)[d]] * 4 + x
            send(("RL2", p, d), rrel.at[p, d], rbuf.at[origin, p, half[d]], y_to[d])

    def r_own(p):
        for d in range(2):
            send(("RX", 0, p, d), r_ref.at[yh, p], rbuf.at[col, p], x_to[d])

    def r_across(j, p):
        chunk = ys[(0, 3, 1, 2)[j]] * 4 + x
        for d in range(2):
            send(("RX", j, p, d), rbuf.at[chunk, p], rbuf.at[chunk, p], x_to[d])

    def r_onward(j, p):
        for d in range(2):
            arrive("RX", j, p, d)
            chunk = ys[(0, 3, 1, 2)[j]] * 4 + xs[(3, 1)[d]]
            part = rbuf.at[chunk, p, half[d]]
            send(("RF", j, p, d), part, part, x_to[d])

    def t_start(ph):
        for d in range(2):
            rows = pl.ds(d * 128, 128)
            send(("TL1", ph, d), t_ref.at[:, pars[ph], xs[2], rows], trel.at[ph, d], x_to[d])
        for d in range(2):
            send(("TD", ph, d), t_ref.at[:, pars[ph], xs[(1, 3)[d]]], tbuf.at[ph, x], x_to[d])

    def t_relay(ph):
        for d in range(2):
            arrive("TL1", ph, d)
            rows = pl.ds(d * 128, 128)
            send(("TL2", ph, d), trel.at[ph, d], tbuf.at[ph, xs[(3, 1)[d]], :, rows], x_to[d])

    def t_done(ph):
        own_t[ph].wait()
        for d in range(2):
            arrive("TD", ph, d)
            arrive("TL2", ph, d)

    def z_send(o, s):
        for d in range(2):
            if s:
                arrive("Z", o, s - 1, d)
            part = sbuf.at[block[o], core, zs[(-s, s)[d]]]
            if s == 3:
                part = part.at[d]
            send(("Z", o, s, d), part, part, z_to[d])

    def s_share(o):
        for d in range(2):
            arrive("Z", o, 3, d)
        part = sbuf.at[block[o], core]
        send(("SC", o), part, part, twin)

    def s_ready(o):
        arrive("SC", o)
        j = (block[o] * 4 + x) * 2
        for k in range(16):
            for c in range(2):
                m = jnp.full((64, 128), sp[k, j + c].astype(jnp.float32)).astype(jnp.bfloat16)
                for b in range(2):
                    seff[o, k * 128 + b * 64 : k * 128 + b * 64 + 64, c * 128 : c * 128 + 128] = (
                        sbuf[block[o], b, k // 2, k % 2, :, c * 128 : c * 128 + 128] * m
                    )

    def r_ready(p):
        for j in range(4):
            for d in range(2):
                arrive("RF", j, p, d)
        for q in range(H // BLK):
            rows = slice(q * BLK, q * BLK + BLK)
            for k in range(16):
                m = rp[yh * 4 + p * (H // BLK) + q, k].astype(jnp.float32)
                m = jnp.full((BLK, BLK), m).astype(jnp.bfloat16)
                reff[p, rows, k * BLK : k * BLK + BLK] = rbuf[k, p, rows] * m

    def compute(p, o, dst):
        ph = 1 if o in (0, 3) else 0
        i = lax.div(block[o], 2)
        paths = jnp.dot(reff[p], seff[o], preferred_element_type=jnp.float32)
        for h in range(H // BLK):
            q = p * (H // BLK) + h
            for c in range(2):
                m = tp[(block[o] * 4 + x) * 2 + c, lax.rem(row, 8) * 16 + yh * 4 + q]
                t = tbuf[ph, q, i, c * BLK : c * BLK + BLK].astype(jnp.float32).T
                t = t * m.astype(jnp.float32)
                rows, cols = slice(h * BLK, h * BLK + BLK), slice(c * BLK, c * BLK + BLK)
                dst[rows, cols] = (paths[rows, cols] * t).astype(jnp.bfloat16)

    def near(p, o):
        compute(p, o, obuf.at[o, p])
        send(("OD", p, o), obuf.at[o, p], out_ref.at[yh, p], y_to[o - 1])

    def far(p):
        compute(p, 3, obuf.at[3, p])
        for d in range(2):
            send(("OL1", p, d), obuf.at[3, p, half[d]], orel.at[p, d], y_to[d])

    def out_relay(p):
        for d in range(2):
            arrive("OL1", p, d)
            send(("OL2", p, d), orel.at[p, d], out_ref.at[ys[(3, 1)[d]], p, half[d]], y_to[d])

    send(("SP",), s_ref, sbuf.at[yh, core, z, yl], pair)
    r_legs(0)
    r_own(0)
    r_own(1)
    t_start(0)
    own_s.wait()
    arrive("SP")
    for d in range(2):
        mine = sbuf.at[yh, core, z]
        send(("S2", d), mine, mine, y_to[d])
    z_send(0, 0)
    r_direct(0)
    r_legs(1)
    r_onward(0, 0)
    r_relay(0)
    r_onward(0, 1)
    z_send(0, 1)
    for d in range(2):
        arrive("S2", d)
        part = sbuf.at[block[(2, 1)[d]], core, z, d]
        send(("SF", d), part, part, y_to[d])
    z_send(1, 0)
    z_send(2, 0)
    r_direct(1)
    z_send(0, 2)
    t_relay(0)
    for d in range(2):
        arrive("RY", 0, d)
        r_across(1 + d, 0)
    z_send(0, 3)
    for d in range(2):
        arrive("RL2", 0, d)
    r_across(3, 0)
    z_send(1, 1)
    r_relay(1)
    for d in range(2):
        arrive("SF", d)
    z_send(2, 1)
    z_send(3, 0)
    r_onward(1, 0)
    z_send(1, 2)
    r_onward(2, 0)
    s_share(0)
    z_send(2, 2)
    r_onward(3, 0)
    z_send(1, 3)
    for d in range(2):
        arrive("RY", 1, d)
        r_across(1 + d, 1)
    z_send(2, 3)
    z_send(3, 1)
    s_share(1)
    for c in own_r + masks:
        c.wait()
    r_ready(0)
    for d in range(2):
        arrive("RL2", 1, d)
    r_across(3, 1)
    t_done(0)
    z_send(3, 2)
    s_share(2)
    s_ready(1)
    near(0, 1)
    t_start(1)
    r_onward(1, 1)
    s_ready(2)
    near(0, 2)
    z_send(3, 3)
    r_onward(2, 1)
    r_onward(3, 1)
    s_share(3)
    t_relay(1)
    s_ready(0)
    r_ready(1)
    near(1, 1)
    near(1, 2)
    s_ready(3)
    t_done(1)
    far(0)
    far(1)
    out_relay(0)
    out_relay(1)
    for p in range(PASSES):
        compute(p, 0, out_ref.at[yh, p])
    for p in range(PASSES):
        for d in range(2):
            arrive("OD", p, 1 + d)
            arrive("OL2", p, d)
    for copy in sent.values():
        copy.wait_send()


def body(r_vals, s_vals, t_vals, r_pattern, s_pattern, t_pattern):
    any_space = pl.BlockSpec(memory_space=pl.ANY)
    bf16 = jnp.bfloat16
    out = pl.pallas_call(
        kernel,
        out_shape=jax.ShapeDtypeStruct((4, PASSES, H, 256), bf16),
        in_specs=[any_space] * 6,
        out_specs=pl.BlockSpec(memory_space=pltpu.VMEM),
        scratch_shapes=[
            pltpu.VMEM((16, PASSES, H, BLK), bf16),
            pltpu.VMEM((PASSES, 2, H // 2, BLK), bf16),
            pltpu.VMEM((4, 2, 8, 2, 64, 256), bf16),
            pltpu.VMEM((2, 4, 2, 256, BLK), bf16),
            pltpu.VMEM((2, 2, 2, 128, BLK), bf16),
            pltpu.VMEM((4, PASSES, H, 256), bf16),
            pltpu.VMEM((PASSES, 2, H // 2, 256), bf16),
            pltpu.VMEM((PASSES, H, 2048), bf16),
            pltpu.VMEM((4, 2048, 256), bf16),
            pltpu.SMEM((16, 16), jnp.int32),
            pltpu.SMEM((16, 32), jnp.int32),
            pltpu.SMEM((32, 128), jnp.int32),
            pltpu.SemaphoreType.DMA((SEMS,)),
            pltpu.SemaphoreType.DMA((SEMS,)),
            pltpu.SemaphoreType.DMA((8,)),
        ],
        compiler_params=pltpu.CompilerParams(
            collective_id=0, has_side_effects=True, vmem_limit_bytes=48 << 20
        ),
    )(
        r_vals.reshape(4, PASSES, H, BLK),
        s_vals,
        t_vals.reshape(2, 2, 4, 256, BLK),
        r_pattern,
        s_pattern,
        t_pattern,
    )
    return out.reshape(2048, 256)


def solution(mesh):
    placed = (P("row", "col"), P("row", "col"), P(None, ("row", "col")), P(), P(), P())
    return jax.shard_map(
        body, mesh=mesh, in_specs=placed, out_specs=P("row", "col"), check_vma=False
    )
```

time: 185 us -> 80.3 us (0.43)
  the two profiles are of different devices: /device:TPU:1 before, /device:TPU:72 now
where the time goes in v1:
time: 80.3 us; the launch traced here: 80.1 us
  Pallas kernels  75.9 us (95%)
  local copies, waits for them, and re-layouts  4.16 us (5%)
    pallas_call x1, Pallas kernels, body(): pl.pallas_call(kernel, out_shape=jax.ShapeDtypeStruct((4, PASSES, H, 256)...  75.9 us
    unnamed x12, local copies, waits for them, and re-layouts  4.16 us

profile of v1, /device:TPU:72, one launch (start us, length us, event | category | flops | bytes accessed | tf_op | source)
XLA Modules:
  0.0 80.1 jit_solution(2045423572551766098)
XLA Ops:
  0.0 0.0 copy-start.2
  0.0 0.0 copy-start.3
  0.0 0.0 copy-start.4
  0.0 0.9 %copy.7.rp_ref = s32[512,16]{1,0:T(8,128)S(1)} copy(s32[512,16]{0,1:T(8,128)} %param.9) | data formatting | bytes 65536 | tf_op args[3]
  0.9 0.0 copy-done.2
  0.9 0.0 copy-done.3
  0.9 0.0 copy-done.4
  1.0 0.0 copy-start
  1.0 1.2 %copy-done = bf16[4096,128]{1,0:T(8,128)(2,1)S(1)} copy-done((bf16[4096,128]{1,0:T(8,128)(2,1)S(1)}, bf16[4096,128]{1,0:T(8,128)(2,1)}, u32[]{:S(2)}) %copy-start) | copy-done | bytes 1048600
  2.2 0.0 copy-start.1
  2.2 1.0 %copy-done.1 = bf16[2048,128]{1,0:T(8,128)(2,1)S(1)} copy-done((bf16[2048,128]{1,0:T(8,128)(2,1)S(1)}, bf16[2048,128]{1,0:T(8,128)(2,1)}, u32[]{:S(2)}) %copy-start.1) | copy-done | bytes 524312
  3.2 75.9 %shard_map.64 = bf16[4,2,256,256]{3,2,1,0:T(8,128)(2,1)S(1)} custom-call(bf16[4,2,256,128]{3,2,1,0:T(8,128)(2,1)S(1)} %bitcast.5, bf16[64,256]{1,0:T(8,128)(2,1)S(1)} %copy-done.3, bf16[2,2,4,256,128]{4,3,2,1,0:T(8,128)(2,1)S(1)} %bitcast.4, s32[512,16]{1,0:T(8,128)S(1)} %copy.7.rp_ref, s32[16,32]{1,0:T(8,128)S(1)} %copy-done.4, s32[32,512]{1,0:T(8,128)S(1)} %copy-done.2), custom_call_target="tpu_custom_call" | custom-call | tf_op jit(solution)/shard_map/pallas_call | solution.py:277
  79.1 1.0 %copy.9 = bf16[2048,256]{1,0:T(8,128)(2,1)} copy(bf16[2048,256]{1,0:T(8,128)(2,1)S(1)} %bitcast.3) | data formatting | bytes 2097152
Async XLA Ops:
  0.0 0.9 %copy-start.2 = (s32[32,512]{1,0:T(8,128)S(1)}, s32[32,512]{1,0:T(8,128)}, u32[]{:S(2)}) copy-start(s32[32,512]{1,0:T(8,128)} %tp_ref.1) | copy-start | bytes 196612
  0.0 0.9 %copy-start.3 = (bf16[64,256]{1,0:T(8,128)(2,1)S(1)}, bf16[64,256]{1,0:T(8,128)(2,1)}, u32[]{:S(2)}) copy-start(bf16[64,256]{1,0:T(8,128)(2,1)} %s_ref.1) | copy-start | bytes 98308
  0.0 0.9 %copy-start.4 = (s32[16,32]{1,0:T(8,128)S(1)}, s32[16,32]{1,0:T(8,128)}, u32[]{:S(2)}) copy-start(s32[16,32]{1,0:T(8,128)} %sp_ref.1) | copy-start | bytes 6148
  1.0 1.2 %copy-start = (bf16[4096,128]{1,0:T(8,128)(2,1)S(1)}, bf16[4096,128]{1,0:T(8,128)(2,1)}, u32[]{:S(2)}) copy-start(bf16[4096,128]{1,0:T(8,128)(2,1)} %param.8) | copy-start | bytes 3145732
  2.2 1.0 %copy-start.1 = (bf16[2048,128]{1,0:T(8,128)(2,1)S(1)}, bf16[2048,128]{1,0:T(8,128)(2,1)}, u32[]{:S(2)}) copy-start(bf16[2048,128]{1,0:T(8,128)(2,1)} %param.6) | copy-start | bytes 1572868

commit v2 on v0

v2 whole, which is shorter than its diff:
```python
import jax
import jax.numpy as jnp
from jax import lax
from jax.experimental import pallas as pl
from jax.experimental.pallas import tpu as pltpu
from jax.sharding import PartitionSpec as P

MESH = pl.DeviceIdType.MESH
BLK = 128
PASSES = 2
H = 512 // PASSES
UNITS = {0: (2,), 1: (0, 1), 2: (0, 1), 3: (0, 1)}
ORDER = (
    ("SU", 1, 1, 1), ("SU", 1, 1, 0), ("TL1", 0, 0), ("SU", 2, 0, 1), ("RX", 0, 0, 1),
    ("SU", 2, 1, 1), ("TD", 0, 0), ("RX", 0, 1, 0), ("SU", 1, 0, 0), ("SU", 2, 1, 0),
    ("SU", 2, 0, 0), ("SU", 1, 0, 1), ("RL1", 0, 0), ("TL1", 0, 1), ("RL1", 0, 1), ("RY", 0, 1),
    ("RY", 0, 0), ("RL1", 1, 0), ("TD", 0, 1), ("Z", 2, 1, 0, 1), ("RX", 0, 0, 0),
    ("Z", 2, 1, 0, 0), ("RF", 0, 0, 1), ("Z", 1, 0, 0, 1), ("TL2", 0, 1), ("SU", 3, 1, 1),
    ("RL1", 1, 1), ("Z", 1, 0, 0, 0), ("SU", 3, 0, 1), ("Z", 1, 1, 0, 1), ("Z", 1, 1, 0, 0),
    ("TL1", 1, 0), ("TL2", 0, 0), ("Z", 2, 0, 0, 1), ("RL2", 0, 1), ("Z", 2, 0, 0, 0),
    ("Z", 2, 1, 1, 0), ("Z", 2, 1, 1, 1), ("RX", 0, 1, 1), ("RL2", 0, 0), ("SU", 3, 0, 0),
    ("Z", 1, 0, 1, 1), ("Z", 1, 0, 1, 0), ("RF", 0, 1, 0), ("RY", 1, 0), ("RX", 2, 0, 0),
    ("RX", 2, 0, 1), ("RY", 1, 1), ("RF", 0, 0, 0), ("RX", 1, 0, 0), ("SU", 3, 1, 0),
    ("Z", 1, 1, 1, 1), ("Z", 2, 0, 1, 1), ("Z", 2, 0, 1, 0), ("TL1", 1, 1), ("Z", 1, 1, 1, 0),
    ("RL2", 1, 0), ("Z", 2, 1, 2, 0), ("Z", 2, 1, 2, 1), ("RX", 1, 0, 1), ("TL2", 1, 0),
    ("Z", 1, 0, 2, 1), ("Z", 1, 0, 2, 0), ("Z", 3, 1, 0, 0), ("SU", 0, 0, 0), ("Z", 3, 1, 0, 1),
    ("RX", 3, 0, 0), ("RX", 3, 0, 1), ("Z", 1, 1, 2, 1), ("SU", 0, 0, 1), ("RL2", 1, 1),
    ("Z", 2, 0, 2, 0), ("Z", 1, 1, 2, 0), ("Z", 2, 0, 2, 1), ("Z", 2, 1, 3, 0), ("Z", 1, 0, 3, 1),
    ("RF", 2, 0, 1), ("RF", 1, 0, 0), ("RF", 2, 0, 0), ("Z", 1, 0, 3, 0), ("Z", 2, 1, 3, 1),
    ("RF", 1, 0, 1), ("RX", 2, 1, 0), ("RX", 2, 1, 1), ("Z", 3, 0, 0, 1), ("Z", 3, 0, 0, 0),
    ("RF", 3, 0, 1), ("RF", 3, 0, 0), ("Z", 1, 1, 3, 1), ("Z", 2, 0, 3, 1), ("Z", 2, 0, 3, 0),
    ("Z", 3, 1, 1, 0), ("RX", 1, 1, 1), ("RX", 1, 1, 0), ("Z", 0, 2, 0, 1), ("SC", 2, 1),
    ("RX", 3, 1, 1), ("RX", 3, 1, 0), ("TL2", 1, 1), ("Z", 1, 1, 3, 0), ("RF", 0, 1, 1),
    ("SC", 1, 0), ("Z", 3, 1, 1, 1), ("RF", 2, 1, 0), ("Z", 3, 0, 1, 0), ("Z", 3, 0, 1, 1),
    ("RF", 2, 1, 1), ("SR", 2, 1), ("Z", 0, 2, 0, 0), ("RR", 0), ("SC", 2, 0), ("SR", 1, 0),
    ("C", 0, 1, 0), ("OD", 0, 1, 0), ("C", 0, 2, 1), ("RF", 1, 1, 1), ("OD", 0, 2, 1),
    ("Z", 3, 1, 2, 0), ("RF", 1, 1, 0), ("SC", 1, 1), ("Z", 3, 1, 2, 1), ("RF", 3, 1, 0),
    ("RF", 3, 1, 1), ("SR", 2, 0), ("Z", 3, 0, 2, 1), ("Z", 3, 0, 2, 0), ("TD", 1, 0), ("SR", 1, 1),
    ("C", 0, 1, 1), ("C", 0, 2, 0), ("OD", 0, 1, 1), ("OD", 0, 2, 0), ("Z", 3, 1, 3, 0),
    ("TD", 1, 1), ("Z", 3, 1, 3, 1), ("RR", 1), ("Z", 3, 0, 3, 1), ("Z", 3, 0, 3, 0),
    ("C", 1, 2, 0), ("OD", 1, 2, 0), ("C", 1, 1, 1), ("OD", 1, 1, 1), ("C", 1, 2, 1),
    ("Z", 0, 2, 1, 1), ("C", 1, 1, 0), ("SC", 3, 1), ("OD", 1, 2, 1), ("OD", 1, 1, 0), ("SC", 3, 0),
    ("SR", 3, 1), ("Z", 0, 2, 1, 0), ("C", 0, 3, 1), ("C", 1, 3, 1), ("Z", 0, 2, 2, 1),
    ("SR", 3, 0), ("C", 1, 3, 0), ("OL1", 1, 0), ("C", 0, 3, 0), ("OL1", 0, 1), ("OL1", 1, 1),
    ("OL1", 0, 0), ("Z", 0, 2, 2, 0), ("Z", 0, 2, 3, 1), ("OL2", 0, 1), ("OL2", 1, 0),
    ("Z", 0, 2, 3, 0), ("OL2", 1, 1), ("OL2", 0, 0), ("SC", 0, 2), ("SR", 0, 2), ("C", 0, 0, 2),
    ("C", 1, 0, 2),
)


def kernel(
    r_ref, s_ref, t_ref, rp_ref, sp_ref, tp_ref, out_ref,
    rbuf, rrel, sbuf, tbuf, trel, obuf, orel, reff, seff, rp, sp, tp, ssem, rsem, usem, lsem,
):
    row, col = lax.axis_index("row"), lax.axis_index("col")
    z, yl, core = lax.div(row, 4), lax.rem(lax.div(row, 2), 2), lax.rem(row, 2)
    yh, x = lax.div(col, 4), lax.rem(col, 4)
    xs = [lax.rem(x + d, 4) for d in range(4)]
    ys = [lax.rem(yh + d, 4) for d in range(4)]
    zs = [lax.rem(z + d, 8) for d in range(8)]
    low = yl * 2 + core
    x_to = [(row, yh * 4 + xs[1]), (row, yh * 4 + xs[3])]
    y_to = [(row, ys[1] * 4 + x), (row, ys[3] * 4 + x)]
    z_to = [(zs[1] * 4 + low, col), (zs[7] * 4 + low, col)]
    pair = (z * 4 + (1 - yl) * 2 + core, col)
    twin = (row + 1 - 2 * core, col)
    s_to = {
        (o, q): (z * 4 + q * 2 + core, ys[d] * 4 + x) for o, d in ((1, 3), (2, 1), (3, 2)) for q in range(2)
    }
    par = lax.rem(yh, 2)
    pars = [1 - par, par]
    block = [yh, ys[1], ys[3], ys[2]]
    half = [pl.ds(0, H // 2), pl.ds(H // 2, H // 2)]

    sent, seen, local = {}, set(), {}

    def send(name, src, dst, device, arrival=None):
        n = len(sent)
        sent[name] = pltpu.make_async_remote_copy(
            src_ref=src, dst_ref=dst, send_sem=ssem.at[n],
            recv_sem=rsem.at[n] if arrival is None else usem.at[arrival],
            device_id=device, device_id_type=MESH,
        )
        sent[name].start()

    def need(*name):
        if name not in seen:
            seen.add(name)
            sent[name].wait_recv()

    def here(name):
        if name not in seen:
            seen.add(name)
            local[name].wait()

    def fetch(name, src, dst):
        local[name] = pltpu.make_async_copy(src, dst, lsem.at[len(local)])
        local[name].start()

    def cols(u):
        return slice(0, 256) if u == 2 else slice(u * BLK, u * BLK + BLK)

    def halves(u):
        return (0, 1) if u == 2 else (u,)

    def SU(o, q, c):
        src, dst = s_ref.at[:, cols(c)], sbuf.at[yh, c, core, z, yl]
        if o:
            send(("SU", o, q, c), src, dst, s_to[o, q], (o * 2 + yl) * 2 + c)
        else:
            send(("SU", o, q, c), src, dst, pair, c)

    def s_came(o, c):
        for q in range(2 if o else 1):
            if ("SU", o, q, c) in seen:
                continue
            seen.add(("SU", o, q, c))
            part = sbuf.at[block[o], c, core, z, q]
            pltpu.make_async_remote_copy(
                src_ref=part, dst_ref=part, send_sem=ssem.at[0], recv_sem=usem.at[(o * 2 + q) * 2 + c],
                device_id=pair, device_id_type=MESH,
            ).wait_recv()

    def Z(o, u, s, d):
        if s:
            need("Z", o, u, s - 1, d)
        else:
            for c in halves(u):
                s_came(o, c)
                if o == 0:
                    here(("S", c))
        part = sbuf.at[block[o], slice(0, 2) if u == 2 else u, core, zs[(-s, s)[d]]]
        if s == 3:
            part = part.at[:, d] if u == 2 else part.at[d]
        send(("Z", o, u, s, d), part, part, z_to[d])

    def SC(o, u):
        for d in range(2):
            for s in range(4):
                need("Z", o, u, s, d)
        part = sbuf.at[block[o], slice(0, 2) if u == 2 else u, core]
        send(("SC", o, u), part, part, twin)

    def SR(o, u):
        need("SC", o, u)
        here(("M", 1))
        j = (block[o] * 4 + x) * 2
        for k in range(16):
            for c in halves(u):
                m = jnp.full((64, BLK), sp[k, j + c].astype(jnp.float32)).astype(jnp.bfloat16)
                for b in range(2):
                    rows = slice(k * 128 + b * 64, k * 128 + b * 64 + 64)
                    seff[o, rows, cols(c)] = sbuf[block[o], c, b, k // 2, k % 2] * m

    def RL1(p, d):
        send(("RL1", p, d), r_ref.at[ys[2], p, half[d]], rrel.at[p, d], y_to[d])

    def RY(p, d):
        send(("RY", p, d), r_ref.at[ys[(1, 3)[d]], p], rbuf.at[col, p], y_to[d])

    def RL2(p, d):
        need("RL1", p, d)
        send(("RL2", p, d), rrel.at[p, d], rbuf.at[ys[(3, 1)[d]] * 4 + x, p, half[d]], y_to[d])

    def RX(j, p, d):
        part = rbuf.at[ys[(0, 3, 1, 2)[j]] * 4 + x, p]
        if j == 0:
            send(("RX", j, p, d), r_ref.at[yh, p], part, x_to[d])
            return
        if j == 3:
            need("RL2", p, 0)
            need("RL2", p, 1)
        else:
            need("RY", p, j - 1)
        send(("RX", j, p, d), part, part, x_to[d])

    def RF(j, p, d):
        need("RX", j, p, d)
        part = rbuf.at[ys[(0, 3, 1, 2)[j]] * 4 + xs[(3, 1)[d]], p, half[d]]
        send(("RF", j, p, d), part, part, x_to[d])

    def RR(p):
        here(("R", p))
        here(("M", 0))
        for d in range(2):
            need("RY", p, d)
            need("RL2", p, d)
            for j in range(4):
                need("RX", j, p, d)
                need("RF", j, p, d)
        for q in range(H // BLK):
            rows = slice(q * BLK, q * BLK + BLK)
            for k in range(16):
                m = rp[k, lax.rem(row, 8) * 16 + yh * 4 + p * (H // BLK) + q].astype(jnp.float32)
                m = jnp.full((BLK, BLK), m).astype(jnp.bfloat16)
                reff[p, rows, k * BLK : k * BLK + BLK] = rbuf[k, p, rows] * m

    def TL1(ph, d):
        rows = pl.ds(d * BLK, BLK)
        send(("TL1", ph, d), t_ref.at[:, pars[ph], xs[2], rows], trel.at[ph, d], x_to[d])

    def TD(ph, d):
        send(("TD", ph, d), t_ref.at[:, pars[ph], xs[(1, 3)[d]]], tbuf.at[ph, x], x_to[d])

    def TL2(ph, d):
        need("TL1", ph, d)
        rows = pl.ds(d * BLK, BLK)
        send(("TL2", ph, d), trel.at[ph, d], tbuf.at[ph, xs[(3, 1)[d]], :, rows], x_to[d])

    def C(p, o, u):
        ph = 1 if o in (0, 3) else 0
        here(("T", ph))
        here(("M", 2))
        for d in range(2):
            need("TD", ph, d)
            need("TL2", ph, d)
        i = lax.div(block[o], 2)
        dst = obuf.at[o, p]
        paths = jnp.dot(reff[p], seff[o, :, cols(u)], preferred_element_type=jnp.float32)
        for h in range(H // BLK):
            q = p * (H // BLK) + h
            for n, c in enumerate(halves(u)):
                m = tp[(block[o] * 4 + x) * 2 + c, lax.rem(row, 8) * 16 + yh * 4 + q]
                t = tbuf[ph, q, i, cols(c)].astype(jnp.float32).T * m.astype(jnp.float32)
                rows = slice(h * BLK, h * BLK + BLK)
                dst[rows, cols(c)] = (paths[rows, cols(n)] * t).astype(jnp.bfloat16)

    def OD(p, o, u):
        send(
            ("OD", p, o, u), obuf.at[o, p, :, cols(u)], out_ref.at[yh, p, :, cols(u)], y_to[o - 1]
        )

    def OL1(p, d):
        send(("OL1", p, d), obuf.at[3, p, half[d]], orel.at[p, d], y_to[d])

    def OL2(p, d):
        need("OL1", p, d)
        send(("OL2", p, d), orel.at[p, d], out_ref.at[ys[(3, 1)[d]], p, half[d]], y_to[d])

    barrier = pltpu.get_barrier_semaphore()
    peers = (*x_to, *z_to, pair, twin, *s_to.values())
    for device in peers:
        pl.semaphore_signal(barrier, inc=1, device_id=device, device_id_type=MESH)
    for c in range(2):
        fetch(("S", c), s_ref.at[:, cols(c)], sbuf.at[yh, c, core, z, yl])
    for p in range(PASSES):
        fetch(("R", p), r_ref.at[yh, p], rbuf.at[col, p])
    for ph in range(2):
        fetch(("T", ph), t_ref.at[:, pars[ph], x], tbuf.at[ph, x])
    lanes = pl.ds(pl.multiple_of(lax.div(row, 8) * BLK, BLK), BLK)
    fetch(("M", 0), rp_ref.at[:, lanes], rp)
    fetch(("M", 1), sp_ref, sp)
    fetch(("M", 2), tp_ref.at[:, lanes], tp)
    pl.semaphore_wait(barrier, len(peers))

    steps = dict(
        SU=SU, Z=Z, SC=SC, SR=SR, RL1=RL1, RY=RY, RL2=RL2, RX=RX, RF=RF, RR=RR,
        TL1=TL1, TD=TD, TL2=TL2, C=C, OD=OD, OL1=OL1, OL2=OL2,
    )
    for step, *where in ORDER:
        steps[step](*where)
    for p in range(PASSES):
        fetch(("O", p), obuf.at[0, p], out_ref.at[yh, p])
    for p in range(PASSES):
        here(("O", p))
    for name in sent:
        if name[0] in ("OD", "OL2"):
            need(*name)
    for copy in sent.values():
        copy.wait_send()


def body(r_vals, s_vals, t_vals, r_pattern, s_pattern, t_pattern):
    hbm = pl.BlockSpec(memory_space=pltpu.HBM)
    bf16 = jnp.bfloat16
    out = pl.pallas_call(
        kernel,
        out_shape=jax.ShapeDtypeStruct((4, PASSES, H, 256), bf16),
        in_specs=[hbm] * 6,
        out_specs=hbm,
        scratch_shapes=[
            pltpu.VMEM((16, PASSES, H, BLK), bf16),
            pltpu.VMEM((PASSES, 2, H // 2, BLK), bf16),
            pltpu.VMEM((4, 2, 2, 8, 2, 64, BLK), bf16),
            pltpu.VMEM((2, 4, 2, 256, BLK), bf16),
            pltpu.VMEM((2, 2, 2, BLK, BLK), bf16),
            pltpu.VMEM((4, PASSES, H, 256), bf16),
            pltpu.VMEM((PASSES, 2, H // 2, 256), bf16),
            pltpu.VMEM((PASSES, H, 2048), bf16),
            pltpu.VMEM((4, 2048, 256), bf16),
            pltpu.SMEM((16, BLK), jnp.int32),
            pltpu.SMEM((16, 32), jnp.int32),
            pltpu.SMEM((32, BLK), jnp.int32),
            pltpu.SemaphoreType.DMA((len(ORDER),)),
            pltpu.SemaphoreType.DMA((len(ORDER),)),
            pltpu.SemaphoreType.DMA((16,)),
            pltpu.SemaphoreType.DMA((9 + PASSES,)),
        ],
        compiler_params=pltpu.CompilerParams(
            collective_id=0, has_side_effects=True, vmem_limit_bytes=67043328
        ),
    )(
        r_vals.reshape(4, PASSES, H, BLK),
        s_vals,
        t_vals.reshape(2, 2, 4, 256, BLK),
        r_pattern.T,
        s_pattern,
        t_pattern,
    )
    return out.reshape(2048, 256)


def solution(mesh):
    placed = (P("row", "col"), P("row", "col"), P(None, ("row", "col")), P(), P(), P())
    return jax.shard_map(
        body, mesh=mesh, in_specs=placed, out_specs=P("row", "col"), check_vma=False
    )
```

time: 185 us -> 72.8 us (0.39)
  waiting for transfers between devices: 87.1 us -> 0 us
  Pallas kernels: 0 us -> 70.4 us
  blocking collectives: 43.5 us -> 0 us
  local copies, waits for them, and re-layouts: 18.5 us -> 2.26 us
  starting transfers between devices: 15.4 us -> 0 us
  between operations: 13.5 us -> 0.01 us
  matrix products: 3.8 us -> 0 us
  other arithmetic: 2.43 us -> 0 us
    pallas_call x0 -> x1, Pallas kernels: none -> 70.4 us  [body(): pl.pallas_call(kernel, out_shape=jax.ShapeDtypeStruct((4, PASSES, H, 256)...]
    all_gather x1 -> x0, waiting for transfers between devices: 60.9 us -> none  [body(): r_all = lax.all_gather(r_vals, 'col', axis=1, tiled=True)]
    all_to_all x1 -> x0, blocking collectives: 43.5 us -> none  [body(): lax.all_to_all(t_vals, 'col', split_axis=0, concat_axis=1, tiled=True)]
    all_to_all x1 -> x0, waiting for transfers between devices: 25.5 us -> none  [sent_to_all(): lax.all_to_all(jnp.broadcast_to(value[None], (peers, *value.shape)), axis...]
    broadcast_in_dim x6 -> x0, local copies, waits for them, and re-layouts: 16.8 us -> none  [the longest x2 9.03 us: body(): r_mask = jnp.repeat(jnp.repeat(r_rows, BLK, axis=0), BLK, axis=1)]
    all_to_all x1 -> x0, starting transfers between devices: 15.4 us -> none  [sent_to_all(): lax.all_to_all(jnp.broadcast_to(value[None], (peers, *value.shape)), axis...]
    dot_general x1 -> x0, matrix products: 3.8 us -> none  [body(): jnp.dot(r_all * r_mask, s_all * s_mask, preferred_element_type=jnp.float32)]
    convert_element_type x3 -> x0, other arithmetic: 2.35 us -> none  [the longest x1 0.8 us: body(): lax.dynamic_slice_in_dim(t_tiles, row_index * a_tiles, a_tiles, 1)]
  transfers between devices with their start and end apart: 2 -> 0, of which waited for: 2 -> 0; matrix products, arithmetic and copies ran while one was open for 3% -> 0% of each run, Pallas kernels for 0% -> 0%
where the time goes in v2:
time: 72.8 us; the launch traced here: 72.7 us
  Pallas kernels  70.4 us (97%)
  local copies, waits for them, and re-layouts  2.26 us (3%)
    pallas_call x1, Pallas kernels, body(): pl.pallas_call(kernel, out_shape=jax.ShapeDtypeStruct((4, PASSES, H, 256)...  70.4 us
    unnamed x1, local copies, waits for them, and re-layouts  2.26 us

profile of v2, /device:TPU:1, one launch (start us, length us, event | category | flops | bytes accessed | tf_op | source)
XLA Modules:
  0.0 72.7 jit_solution(17334061464668635479)
XLA Ops:
  0.0 70.4 %shard_map.64 = bf16[4,2,256,256]{3,2,1,0:T(8,128)(2,1)} custom-call(bf16[4,2,256,128]{3,2,1,0:T(8,128)(2,1)} %bitcast.6, bf16[64,256]{1,0:T(8,128)(2,1)} %s_ref.1, bf16[2,2,4,256,128]{4,3,2,1,0:T(8,128)(2,1)} %bitcast.5, s32[16,512]{1,0:T(8,128)} %bitcast.7, s32[16,32]{1,0:T(8,128)} %sp_ref.1, s32[32,512]{1,0:T(8,128)} %tp_ref.1), custom_call_target="tpu_custom_call" | custom-call | tf_op jit(solution)/shard_map/pallas_call | solution.py:276
  70.4 2.3 %copy.8 = bf16[2048,256]{1,0:T(8,128)(2,1)} copy(bf16[2048,256]{1,0:T(8,128)(2,1)} %bitcast.4) | data formatting | bytes 2097152

commit v3 on v2

--- a/solution.py
+++ b/solution.py
@@ -11,40 +11,42 @@
 H = 512 // PASSES
 UNITS = {0: (2,), 1: (0, 1), 2: (0, 1), 3: (0, 1)}
 ORDER = (
-    ("SU", 1, 1, 1), ("SU", 1, 1, 0), ("TL1", 0, 0), ("SU", 2, 0, 1), ("RX", 0, 0, 1),
-    ("SU", 2, 1, 1), ("TD", 0, 0), ("RX", 0, 1, 0), ("SU", 1, 0, 0), ("SU", 2, 1, 0),
-    ("SU", 2, 0, 0), ("SU", 1, 0, 1), ("RL1", 0, 0), ("TL1", 0, 1), ("RL1", 0, 1), ("RY", 0, 1),
-    ("RY", 0, 0), ("RL1", 1, 0), ("TD", 0, 1), ("Z", 2, 1, 0, 1), ("RX", 0, 0, 0),
-    ("Z", 2, 1, 0, 0), ("RF", 0, 0, 1), ("Z", 1, 0, 0, 1), ("TL2", 0, 1), ("SU", 3, 1, 1),
-    ("RL1", 1, 1), ("Z", 1, 0, 0, 0), ("SU", 3, 0, 1), ("Z", 1, 1, 0, 1), ("Z", 1, 1, 0, 0),
-    ("TL1", 1, 0), ("TL2", 0, 0), ("Z", 2, 0, 0, 1), ("RL2", 0, 1), ("Z", 2, 0, 0, 0),
-    ("Z", 2, 1, 1, 0), ("Z", 2, 1, 1, 1), ("RX", 0, 1, 1), ("RL2", 0, 0), ("SU", 3, 0, 0),
-    ("Z", 1, 0, 1, 1), ("Z", 1, 0, 1, 0), ("RF", 0, 1, 0), ("RY", 1, 0), ("RX", 2, 0, 0),
-    ("RX", 2, 0, 1), ("RY", 1, 1), ("RF", 0, 0, 0), ("RX", 1, 0, 0), ("SU", 3, 1, 0),
-    ("Z", 1, 1, 1, 1), ("Z", 2, 0, 1, 1), ("Z", 2, 0, 1, 0), ("TL1", 1, 1), ("Z", 1, 1, 1, 0),
-    ("RL2", 1, 0), ("Z", 2, 1, 2, 0), ("Z", 2, 1, 2, 1), ("RX", 1, 0, 1), ("TL2", 1, 0),
-    ("Z", 1, 0, 2, 1), ("Z", 1, 0, 2, 0), ("Z", 3, 1, 0, 0), ("SU", 0, 0, 0), ("Z", 3, 1, 0, 1),
-    ("RX", 3, 0, 0), ("RX", 3, 0, 1), ("Z", 1, 1, 2, 1), ("SU", 0, 0, 1), ("RL2", 1, 1),
-    ("Z", 2, 0, 2, 0), ("Z", 1, 1, 2, 0), ("Z", 2, 0, 2, 1), ("Z", 2, 1, 3, 0), ("Z", 1, 0, 3, 1),
-    ("RF", 2, 0, 1), ("RF", 1, 0, 0), ("RF", 2, 0, 0), ("Z", 1, 0, 3, 0), ("Z", 2, 1, 3, 1),
-    ("RF", 1, 0, 1), ("RX", 2, 1, 0), ("RX", 2, 1, 1), ("Z", 3, 0, 0, 1), ("Z", 3, 0, 0, 0),
-    ("RF", 3, 0, 1), ("RF", 3, 0, 0), ("Z", 1, 1, 3, 1), ("Z", 2, 0, 3, 1), ("Z", 2, 0, 3, 0),
-    ("Z", 3, 1, 1, 0), ("RX", 1, 1, 1), ("RX", 1, 1, 0), ("Z", 0, 2, 0, 1), ("SC", 2, 1),
-    ("RX", 3, 1, 1), ("RX", 3, 1, 0), ("TL2", 1, 1), ("Z", 1, 1, 3, 0), ("RF", 0, 1, 1),
-    ("SC", 1, 0), ("Z", 3, 1, 1, 1), ("RF", 2, 1, 0), ("Z", 3, 0, 1, 0), ("Z", 3, 0, 1, 1),
-    ("RF", 2, 1, 1), ("SR", 2, 1), ("Z", 0, 2, 0, 0), ("RR", 0), ("SC", 2, 0), ("SR", 1, 0),
-    ("C", 0, 1, 0), ("OD", 0, 1, 0), ("C", 0, 2, 1), ("RF", 1, 1, 1), ("OD", 0, 2, 1),
-    ("Z", 3, 1, 2, 0), ("RF", 1, 1, 0), ("SC", 1, 1), ("Z", 3, 1, 2, 1), ("RF", 3, 1, 0),
-    ("RF", 3, 1, 1), ("SR", 2, 0), ("Z", 3, 0, 2, 1), ("Z", 3, 0, 2, 0), ("TD", 1, 0), ("SR", 1, 1),
-    ("C", 0, 1, 1), ("C", 0, 2, 0), ("OD", 0, 1, 1), ("OD", 0, 2, 0), ("Z", 3, 1, 3, 0),
-    ("TD", 1, 1), ("Z", 3, 1, 3, 1), ("RR", 1), ("Z", 3, 0, 3, 1), ("Z", 3, 0, 3, 0),
-    ("C", 1, 2, 0), ("OD", 1, 2, 0), ("C", 1, 1, 1), ("OD", 1, 1, 1), ("C", 1, 2, 1),
-    ("Z", 0, 2, 1, 1), ("C", 1, 1, 0), ("SC", 3, 1), ("OD", 1, 2, 1), ("OD", 1, 1, 0), ("SC", 3, 0),
-    ("SR", 3, 1), ("Z", 0, 2, 1, 0), ("C", 0, 3, 1), ("C", 1, 3, 1), ("Z", 0, 2, 2, 1),
-    ("SR", 3, 0), ("C", 1, 3, 0), ("OL1", 1, 0), ("C", 0, 3, 0), ("OL1", 0, 1), ("OL1", 1, 1),
-    ("OL1", 0, 0), ("Z", 0, 2, 2, 0), ("Z", 0, 2, 3, 1), ("OL2", 0, 1), ("OL2", 1, 0),
-    ("Z", 0, 2, 3, 0), ("OL2", 1, 1), ("OL2", 0, 0), ("SC", 0, 2), ("SR", 0, 2), ("C", 0, 0, 2),
-    ("C", 1, 0, 2),
+    ("SU", 1, 0, 0), ("SU", 2, 1, 1), ("TL1", 0, 0), ("TL1", 0, 1), ("SU", 1, 0, 1),
+    ("SU", 2, 0, 1), ("RX", 0, 1, 0), ("RX", 0, 1, 1), ("SU", 1, 1, 1), ("RL1", 0, 0),
+    ("SU", 1, 1, 0), ("RX", 0, 0, 0), ("RX", 0, 0, 1), ("SU", 2, 1, 0), ("RL1", 0, 1),
+    ("SU", 2, 0, 0), ("TL2", 0, 1), ("TL1", 1, 0), ("RY", 0, 0), ("RY", 0, 1), ("Z", 2, 1, 0, 0),
+    ("Z", 2, 1, 0, 1), ("RF", 0, 1, 1), ("RF", 0, 1, 0), ("Z", 1, 1, 0, 0), ("Z", 1, 1, 0, 1),
+    ("TL2", 0, 0), ("TD", 0, 1), ("Z", 1, 0, 0, 0), ("Z", 1, 0, 0, 1), ("RL1", 1, 0), ("RY", 1, 1),
+    ("RF", 0, 0, 0), ("Z", 2, 0, 0, 0), ("Z", 2, 0, 0, 1), ("TD", 0, 0), ("Z", 2, 1, 1, 0),
+    ("Z", 2, 1, 1, 1), ("RL2", 0, 0), ("RF", 0, 0, 1), ("Z", 1, 1, 1, 0), ("Z", 1, 1, 1, 1),
+    ("Z", 1, 0, 1, 0), ("Z", 1, 0, 1, 1), ("RL2", 0, 1), ("SU", 3, 0, 0), ("RX", 2, 0, 1),
+    ("SU", 0, 0, 0), ("Z", 2, 0, 1, 0), ("Z", 2, 0, 1, 1), ("SU", 3, 0, 1), ("SU", 0, 0, 1),
+    ("RX", 1, 0, 0), ("RL1", 1, 1), ("Z", 2, 1, 2, 0), ("Z", 2, 1, 2, 1), ("RX", 1, 0, 1),
+    ("RL2", 1, 0), ("SU", 3, 1, 0), ("Z", 1, 1, 2, 0), ("Z", 1, 1, 2, 1), ("RX", 2, 0, 0),
+    ("Z", 1, 0, 2, 0), ("Z", 1, 0, 2, 1), ("RX", 2, 1, 1), ("RY", 1, 0), ("SU", 3, 1, 1),
+    ("Z", 0, 2, 0, 0), ("Z", 0, 2, 0, 1), ("RH", 0, 0, 0), ("RX", 2, 1, 0), ("RH", 0, 0, 1),
+    ("Z", 2, 0, 2, 1), ("Z", 2, 1, 3, 0), ("RH", 1, 0, 1), ("Z", 2, 0, 2, 0), ("Z", 2, 1, 3, 1),
+    ("RH", 1, 0, 0), ("RF", 2, 0, 1), ("RL2", 1, 1), ("Z", 1, 1, 3, 0), ("Z", 1, 1, 3, 1),
+    ("Z", 1, 0, 3, 0), ("Z", 1, 0, 3, 1), ("RF", 1, 0, 0), ("RF", 1, 0, 1), ("Z", 3, 0, 0, 0),
+    ("Z", 3, 0, 0, 1), ("RF", 3, 0, 0), ("RH", 0, 1, 1), ("Z", 0, 2, 1, 0), ("Z", 0, 2, 1, 1),
+    ("RH", 0, 1, 0), ("RF", 2, 1, 1), ("RF", 2, 0, 0), ("RF", 3, 0, 1), ("SC", 2, 1),
+    ("Z", 2, 0, 3, 0), ("Z", 2, 0, 3, 1), ("RF", 2, 1, 0), ("SC", 1, 1), ("Z", 3, 1, 0, 0),
+    ("Z", 3, 1, 0, 1), ("RX", 1, 1, 1), ("RX", 1, 1, 0), ("SC", 1, 0), ("Z", 3, 0, 1, 0),
+    ("Z", 3, 0, 1, 1), ("RH", 1, 1, 1), ("SR", 2, 1), ("RH", 1, 1, 0), ("Z", 0, 2, 2, 0),
+    ("Z", 0, 2, 2, 1), ("TL1", 1, 1), ("RR", 0), ("SC", 2, 0), ("C", 0, 2, 1), ("SR", 1, 1),
+    ("OD", 0, 2, 1), ("C", 0, 1, 1), ("RF", 3, 1, 0), ("OD", 0, 1, 1), ("Z", 3, 1, 1, 0),
+    ("Z", 3, 1, 1, 1), ("RF", 1, 1, 1), ("Z", 3, 0, 2, 0), ("Z", 3, 0, 2, 1), ("RF", 1, 1, 0),
+    ("RF", 3, 1, 1), ("SR", 2, 0), ("SR", 1, 0), ("TL2", 1, 0), ("C", 0, 1, 0), ("TD", 1, 1),
+    ("C", 0, 2, 0), ("OD", 0, 2, 0), ("OD", 0, 1, 0), ("Z", 0, 2, 3, 0), ("Z", 0, 2, 3, 1),
+    ("TD", 1, 0), ("Z", 3, 1, 2, 0), ("Z", 3, 1, 2, 1), ("Z", 3, 0, 3, 0), ("Z", 3, 0, 3, 1),
+    ("RR", 1), ("C", 1, 1, 1), ("TL2", 1, 1), ("C", 1, 2, 1), ("C", 1, 1, 0), ("OD", 1, 2, 1),
+    ("OD", 1, 1, 1), ("C", 1, 2, 0), ("Z", 3, 1, 3, 0), ("Z", 3, 1, 3, 1), ("SC", 3, 0),
+    ("OD", 1, 2, 0), ("OD", 1, 1, 0), ("SC", 0, 2), ("SR", 3, 0), ("C", 0, 3, 0), ("C", 1, 3, 0),
+    ("SC", 3, 1), ("OL1", 0, 1, 0), ("OL1", 0, 0, 0), ("OL1", 1, 1, 0), ("OL1", 1, 0, 0),
+    ("SR", 0, 2), ("C", 0, 0, 2), ("C", 1, 0, 2), ("SR", 3, 1), ("C", 0, 3, 1), ("C", 1, 3, 1),
+    ("OL1", 0, 0, 1), ("OL1", 0, 1, 1), ("OL1", 1, 0, 1), ("OL1", 1, 1, 1), ("OL2", 0, 0, 0),
+    ("OL2", 0, 1, 0), ("OL2", 1, 0, 0), ("OL2", 1, 1, 0), ("OL2", 0, 0, 1), ("OL2", 0, 1, 1),
+    ("OL2", 1, 0, 1), ("OL2", 1, 1, 1),
 )
 
 
@@ -167,15 +169,19 @@
         if j == 0:
             send(("RX", j, p, d), r_ref.at[yh, p], part, x_to[d])
             return
+        need("RY", p, j - 1)
+        send(("RX", j, p, d), part, part, x_to[d])
+
+    def RH(h, p, d):
+        need("RL2", p, h)
+        part = rbuf.at[ys[2] * 4 + x, p, half[h]]
+        send(("RH", h, p, d), part, part, x_to[d])
+
+    def RF(j, p, d):
         if j == 3:
-            need("RL2", p, 0)
-            need("RL2", p, 1)
+            need("RH", d, p, d)
         else:
-            need("RY", p, j - 1)
-        send(("RX", j, p, d), part, part, x_to[d])
-
-    def RF(j, p, d):
-        need("RX", j, p, d)
+            need("RX", j, p, d)
         part = rbuf.at[ys[(0, 3, 1, 2)[j]] * 4 + xs[(3, 1)[d]], p, half[d]]
         send(("RF", j, p, d), part, part, x_to[d])
 
@@ -186,8 +192,11 @@
             need("RY", p, d)
             need("RL2", p, d)
             for j in range(4):
-                need("RX", j, p, d)
+                if j < 3:
+                    need("RX", j, p, d)
                 need("RF", j, p, d)
+            for h in range(2):
+                need("RH", h, p, d)
         for q in range(H // BLK):
             rows = slice(q * BLK, q * BLK + BLK)
             for k in range(16):
@@ -215,7 +224,7 @@
             need("TD", ph, d)
             need("TL2", ph, d)
         i = lax.div(block[o], 2)
-        dst = obuf.at[o, p]
+        dst = obuf.at[o, p] if o else out_ref.at[yh, p]
         paths = jnp.dot(reff[p], seff[o, :, cols(u)], preferred_element_type=jnp.float32)
         for h in range(H // BLK):
             q = p * (H // BLK) + h
@@ -230,12 +239,14 @@
             ("OD", p, o, u), obuf.at[o, p, :, cols(u)], out_ref.at[yh, p, :, cols(u)], y_to[o - 1]
         )
 
-    def OL1(p, d):
-        send(("OL1", p, d), obuf.at[3, p, half[d]], orel.at[p, d], y_to[d])
-
-    def OL2(p, d):
-        need("OL1", p, d)
-        send(("OL2", p, d), orel.at[p, d], out_ref.at[ys[(3, 1)[d]], p, half[d]], y_to[d])
+    def OL1(p, d, u):
+        part = obuf.at[3, p, half[d], cols(u)]
+        send(("OL1", p, d, u), part, orel.at[p, d, :, cols(u)], y_to[d])
+
+    def OL2(p, d, u):
+        need("OL1", p, d, u)
+        dst = out_ref.at[ys[(3, 1)[d]], p, half[d], cols(u)]
+        send(("OL2", p, d, u), orel.at[p, d, :, cols(u)], dst, y_to[d])
 
     barrier = pltpu.get_barrier_semaphore()
     peers = (*x_to, *z_to, pair, twin, *s_to.values())
@@ -254,15 +265,11 @@
     pl.semaphore_wait(barrier, len(peers))
 
     steps = dict(
-        SU=SU, Z=Z, SC=SC, SR=SR, RL1=RL1, RY=RY, RL2=RL2, RX=RX, RF=RF, RR=RR,
+        SU=SU, Z=Z, SC=SC, SR=SR, RL1=RL1, RY=RY, RL2=RL2, RX=RX, RH=RH, RF=RF, RR=RR,
         TL1=TL1, TD=TD, TL2=TL2, C=C, OD=OD, OL1=OL1, OL2=OL2,
     )
     for step, *where in ORDER:
         steps[step](*where)
-    for p in range(PASSES):
-        fetch(("O", p), obuf.at[0, p], out_ref.at[yh, p])
-    for p in range(PASSES):
-        here(("O", p))
     for name in sent:
         if name[0] in ("OD", "OL2"):
             need(*name)
@@ -277,7 +284,7 @@
         kernel,
         out_shape=jax.ShapeDtypeStruct((4, PASSES, H, 256), bf16),
         in_specs=[hbm] * 6,
-        out_specs=hbm,
+        out_specs=pl.BlockSpec(memory_space=pltpu.VMEM),
         scratch_shapes=[
             pltpu.VMEM((16, PASSES, H, BLK), bf16),
             pltpu.VMEM((PASSES, 2, H // 2, BLK), bf16),
@@ -294,19 +301,19 @@
             pltpu.SemaphoreType.DMA((len(ORDER),)),
             pltpu.SemaphoreType.DMA((len(ORDER),)),
             pltpu.SemaphoreType.DMA((16,)),
-            pltpu.SemaphoreType.DMA((9 + PASSES,)),
+            pltpu.SemaphoreType.DMA((9,)),
         ],
         compiler_params=pltpu.CompilerParams(
-            collective_id=0, has_side_effects=True, vmem_limit_bytes=67043328
+            collective_id=0, has_side_effects=True, vmem_limit_bytes=48 << 20
         ),
-    )(
+    )(*[pltpu.with_memory_space_constraint(a, pltpu.HBM) for a in (
         r_vals.reshape(4, PASSES, H, BLK),
         s_vals,
         t_vals.reshape(2, 2, 4, 256, BLK),
         r_pattern.T,
         s_pattern,
         t_pattern,
-    )
+    )])
     return out.reshape(2048, 256)
 
 

time: 72.8 us -> 69.6 us (0.956); the launches traced: 72.7 us -> 68.4 us
  Pallas kernels: 70.4 us -> 67.4 us
  local copies, waits for them, and re-layouts: 2.26 us -> 0.97 us
    pallas_call x1, Pallas kernels: 70.4 us -> 67.4 us  [body(): pl.pallas_call(kernel, out_shape=jax.ShapeDtypeStruct((4, PASSES, H, 256)...]
    unnamed x1, local copies, waits for them, and re-layouts: 2.26 us -> 0.97 us
where the time goes in v3:
time: 69.6 us; the launch traced here: 68.4 us
  Pallas kernels  67.4 us (97%)
  local copies, waits for them, and re-layouts  0.97 us (1%)
    pallas_call x1, Pallas kernels, body(): pl.pallas_call(kernel, out_shape=jax.ShapeDtypeStruct((4, PASSES, H, 256)...  67.4 us

profile of v3, /device:TPU:1, one launch (start us, length us, event | category | flops | bytes accessed | tf_op | source)
XLA Modules:
  0.0 68.4 jit_solution(17397371798544404299)
XLA Ops:
  0.0 67.4 %shard_map.64 = bf16[4,2,256,256]{3,2,1,0:T(8,128)(2,1)S(1)} custom-call(bf16[4,2,256,128]{3,2,1,0:T(8,128)(2,1)} %bitcast.6, bf16[64,256]{1,0:T(8,128)(2,1)} %s_ref.1, bf16[2,2,4,256,128]{4,3,2,1,0:T(8,128)(2,1)} %bitcast.5, s32[16,512]{1,0:T(8,128)} %bitcast.7, s32[16,32]{1,0:T(8,128)} %sp_ref.1, s32[32,512]{1,0:T(8,128)} %tp_ref.1), custom_call_target="tpu_custom_call" | custom-call | tf_op jit(solution)/shard_map/pallas_call | solution.py:283
  67.4 1.0 %copy.8 = bf16[2048,256]{1,0:T(8,128)(2,1)} copy(bf16[2048,256]{1,0:T(8,128)(2,1)S(1)} %bitcast.4) | data formatting | bytes 2097152

commit v4 on v3

--- a/solution.py
+++ b/solution.py
@@ -10,43 +10,44 @@
 PASSES = 2
 H = 512 // PASSES
 UNITS = {0: (2,), 1: (0, 1), 2: (0, 1), 3: (0, 1)}
+SKIPS = ((1, 0), (2, 0))
 ORDER = (
-    ("SU", 1, 0, 0), ("SU", 2, 1, 1), ("TL1", 0, 0), ("TL1", 0, 1), ("SU", 1, 0, 1),
-    ("SU", 2, 0, 1), ("RX", 0, 1, 0), ("RX", 0, 1, 1), ("SU", 1, 1, 1), ("RL1", 0, 0),
-    ("SU", 1, 1, 0), ("RX", 0, 0, 0), ("RX", 0, 0, 1), ("SU", 2, 1, 0), ("RL1", 0, 1),
-    ("SU", 2, 0, 0), ("TL2", 0, 1), ("TL1", 1, 0), ("RY", 0, 0), ("RY", 0, 1), ("Z", 2, 1, 0, 0),
-    ("Z", 2, 1, 0, 1), ("RF", 0, 1, 1), ("RF", 0, 1, 0), ("Z", 1, 1, 0, 0), ("Z", 1, 1, 0, 1),
-    ("TL2", 0, 0), ("TD", 0, 1), ("Z", 1, 0, 0, 0), ("Z", 1, 0, 0, 1), ("RL1", 1, 0), ("RY", 1, 1),
-    ("RF", 0, 0, 0), ("Z", 2, 0, 0, 0), ("Z", 2, 0, 0, 1), ("TD", 0, 0), ("Z", 2, 1, 1, 0),
-    ("Z", 2, 1, 1, 1), ("RL2", 0, 0), ("RF", 0, 0, 1), ("Z", 1, 1, 1, 0), ("Z", 1, 1, 1, 1),
-    ("Z", 1, 0, 1, 0), ("Z", 1, 0, 1, 1), ("RL2", 0, 1), ("SU", 3, 0, 0), ("RX", 2, 0, 1),
-    ("SU", 0, 0, 0), ("Z", 2, 0, 1, 0), ("Z", 2, 0, 1, 1), ("SU", 3, 0, 1), ("SU", 0, 0, 1),
-    ("RX", 1, 0, 0), ("RL1", 1, 1), ("Z", 2, 1, 2, 0), ("Z", 2, 1, 2, 1), ("RX", 1, 0, 1),
-    ("RL2", 1, 0), ("SU", 3, 1, 0), ("Z", 1, 1, 2, 0), ("Z", 1, 1, 2, 1), ("RX", 2, 0, 0),
-    ("Z", 1, 0, 2, 0), ("Z", 1, 0, 2, 1), ("RX", 2, 1, 1), ("RY", 1, 0), ("SU", 3, 1, 1),
-    ("Z", 0, 2, 0, 0), ("Z", 0, 2, 0, 1), ("RH", 0, 0, 0), ("RX", 2, 1, 0), ("RH", 0, 0, 1),
-    ("Z", 2, 0, 2, 1), ("Z", 2, 1, 3, 0), ("RH", 1, 0, 1), ("Z", 2, 0, 2, 0), ("Z", 2, 1, 3, 1),
-    ("RH", 1, 0, 0), ("RF", 2, 0, 1), ("RL2", 1, 1), ("Z", 1, 1, 3, 0), ("Z", 1, 1, 3, 1),
-    ("Z", 1, 0, 3, 0), ("Z", 1, 0, 3, 1), ("RF", 1, 0, 0), ("RF", 1, 0, 1), ("Z", 3, 0, 0, 0),
-    ("Z", 3, 0, 0, 1), ("RF", 3, 0, 0), ("RH", 0, 1, 1), ("Z", 0, 2, 1, 0), ("Z", 0, 2, 1, 1),
-    ("RH", 0, 1, 0), ("RF", 2, 1, 1), ("RF", 2, 0, 0), ("RF", 3, 0, 1), ("SC", 2, 1),
-    ("Z", 2, 0, 3, 0), ("Z", 2, 0, 3, 1), ("RF", 2, 1, 0), ("SC", 1, 1), ("Z", 3, 1, 0, 0),
-    ("Z", 3, 1, 0, 1), ("RX", 1, 1, 1), ("RX", 1, 1, 0), ("SC", 1, 0), ("Z", 3, 0, 1, 0),
-    ("Z", 3, 0, 1, 1), ("RH", 1, 1, 1), ("SR", 2, 1), ("RH", 1, 1, 0), ("Z", 0, 2, 2, 0),
-    ("Z", 0, 2, 2, 1), ("TL1", 1, 1), ("RR", 0), ("SC", 2, 0), ("C", 0, 2, 1), ("SR", 1, 1),
-    ("OD", 0, 2, 1), ("C", 0, 1, 1), ("RF", 3, 1, 0), ("OD", 0, 1, 1), ("Z", 3, 1, 1, 0),
-    ("Z", 3, 1, 1, 1), ("RF", 1, 1, 1), ("Z", 3, 0, 2, 0), ("Z", 3, 0, 2, 1), ("RF", 1, 1, 0),
-    ("RF", 3, 1, 1), ("SR", 2, 0), ("SR", 1, 0), ("TL2", 1, 0), ("C", 0, 1, 0), ("TD", 1, 1),
-    ("C", 0, 2, 0), ("OD", 0, 2, 0), ("OD", 0, 1, 0), ("Z", 0, 2, 3, 0), ("Z", 0, 2, 3, 1),
-    ("TD", 1, 0), ("Z", 3, 1, 2, 0), ("Z", 3, 1, 2, 1), ("Z", 3, 0, 3, 0), ("Z", 3, 0, 3, 1),
-    ("RR", 1), ("C", 1, 1, 1), ("TL2", 1, 1), ("C", 1, 2, 1), ("C", 1, 1, 0), ("OD", 1, 2, 1),
-    ("OD", 1, 1, 1), ("C", 1, 2, 0), ("Z", 3, 1, 3, 0), ("Z", 3, 1, 3, 1), ("SC", 3, 0),
-    ("OD", 1, 2, 0), ("OD", 1, 1, 0), ("SC", 0, 2), ("SR", 3, 0), ("C", 0, 3, 0), ("C", 1, 3, 0),
-    ("SC", 3, 1), ("OL1", 0, 1, 0), ("OL1", 0, 0, 0), ("OL1", 1, 1, 0), ("OL1", 1, 0, 0),
-    ("SR", 0, 2), ("C", 0, 0, 2), ("C", 1, 0, 2), ("SR", 3, 1), ("C", 0, 3, 1), ("C", 1, 3, 1),
-    ("OL1", 0, 0, 1), ("OL1", 0, 1, 1), ("OL1", 1, 0, 1), ("OL1", 1, 1, 1), ("OL2", 0, 0, 0),
-    ("OL2", 0, 1, 0), ("OL2", 1, 0, 0), ("OL2", 1, 1, 0), ("OL2", 0, 0, 1), ("OL2", 0, 1, 1),
-    ("OL2", 1, 0, 1), ("OL2", 1, 1, 1),
+    ("SU", 1, 0, 0), ("SU", 2, 1, 0), ("SU", 0, 0, 1), ("TD", 0, 0), ("SU", 1, 1, 0), ("RL1", 0, 1),
+    ("RX", 0, 0, 1), ("SU", 2, 0, 1), ("SU", 1, 0, 1), ("SU", 2, 0, 0), ("TL1", 0, 1),
+    ("SU", 2, 1, 1), ("SU", 1, 1, 1), ("RY", 0, 1), ("RX", 0, 1, 0), ("TD", 0, 1), ("TL1", 0, 0),
+    ("RL1", 0, 0), ("SU", 0, 0, 0), ("RY", 0, 0), ("Z", 1, 0, 1, 1), ("Z", 1, 0, 1, 0),
+    ("SU", 3, 0, 1), ("Z", 2, 0, 1, 0), ("Z", 2, 0, 1, 1), ("RL2", 0, 1), ("RF", 0, 1, 0),
+    ("RL1", 1, 1), ("Z", 2, 1, 0, 0), ("Z", 1, 0, 0, 0), ("RX", 0, 1, 1), ("Z", 2, 1, 0, 1),
+    ("RX", 0, 0, 0), ("Z", 1, 1, 0, 1), ("RL2", 0, 0), ("TL2", 0, 0), ("Z", 2, 0, 0, 1),
+    ("RF", 0, 0, 1), ("RL1", 1, 0), ("SU", 3, 1, 1), ("TL2", 0, 1), ("Z", 1, 1, 0, 0),
+    ("Z", 1, 0, 0, 1), ("SU", 3, 1, 0), ("Z", 1, 0, 3, 0), ("SU", 3, 0, 0), ("Z", 1, 0, 3, 1),
+    ("RX", 2, 0, 1), ("Z", 1, 0, 2, 0), ("RX", 1, 0, 0), ("RY", 1, 1), ("RX", 2, 0, 0),
+    ("RY", 1, 0), ("Z", 1, 0, 2, 1), ("Z", 2, 1, 1, 0), ("Z", 2, 0, 3, 0), ("Z", 2, 1, 1, 1),
+    ("RX", 1, 0, 1), ("Z", 1, 1, 1, 1), ("Z", 2, 0, 3, 1), ("Z", 1, 1, 1, 0), ("RH", 1, 0, 1),
+    ("Z", 2, 0, 2, 0), ("TL1", 1, 1), ("Z", 2, 0, 0, 0), ("RH", 0, 0, 0), ("Z", 2, 0, 2, 1),
+    ("RH", 0, 0, 1), ("RL2", 1, 1), ("RH", 1, 0, 0), ("Z", 3, 1, 0, 1), ("Z", 3, 1, 0, 0),
+    ("SC", 1, 0), ("RF", 0, 0, 0), ("RF", 1, 0, 0), ("RL2", 1, 0), ("RF", 2, 0, 1),
+    ("Z", 2, 1, 2, 1), ("Z", 2, 1, 2, 0), ("Z", 1, 1, 2, 1), ("Z", 3, 0, 0, 0), ("Z", 3, 0, 0, 1),
+    ("Z", 1, 1, 2, 0), ("Z", 0, 2, 0, 0), ("RF", 1, 0, 1), ("RF", 2, 0, 0), ("RF", 3, 0, 0),
+    ("RF", 3, 0, 1), ("Z", 0, 2, 0, 1), ("SR", 1, 0), ("SC", 2, 0), ("RX", 2, 1, 0),
+    ("RX", 1, 1, 0), ("RX", 2, 1, 1), ("Z", 2, 1, 3, 1), ("Z", 2, 1, 3, 0), ("Z", 3, 1, 1, 1),
+    ("RX", 1, 1, 1), ("Z", 3, 1, 1, 0), ("Z", 1, 1, 3, 1), ("Z", 3, 0, 1, 1), ("RH", 1, 1, 1),
+    ("Z", 1, 1, 3, 0), ("SR", 2, 0), ("Z", 3, 0, 1, 0), ("RH", 0, 1, 0), ("RR", 0),
+    ("Z", 0, 2, 1, 1), ("Z", 0, 2, 1, 0), ("TL1", 1, 0), ("RF", 0, 1, 1), ("SC", 2, 1),
+    ("C", 0, 2, 0), ("RF", 2, 1, 0), ("RF", 2, 1, 1), ("Z", 3, 1, 2, 0), ("C", 0, 1, 0),
+    ("Z", 3, 1, 2, 1), ("SC", 1, 1), ("RH", 0, 1, 1), ("RF", 1, 1, 0), ("RF", 1, 1, 1),
+    ("Z", 3, 0, 2, 1), ("Z", 3, 0, 2, 0), ("OD", 0, 2, 0), ("OD", 0, 1, 0), ("RF", 3, 1, 0),
+    ("RF", 3, 1, 1), ("RH", 1, 1, 0), ("SR", 2, 1), ("C", 0, 2, 1), ("Z", 0, 2, 2, 1),
+    ("Z", 0, 2, 2, 0), ("OD", 0, 2, 1), ("TD", 1, 0), ("TD", 1, 1), ("SR", 1, 1), ("Z", 3, 1, 3, 0),
+    ("TL2", 1, 0), ("C", 0, 1, 1), ("Z", 3, 1, 3, 1), ("OD", 0, 1, 1), ("Z", 3, 0, 3, 0),
+    ("TL2", 1, 1), ("Z", 3, 0, 3, 1), ("RR", 1), ("C", 1, 1, 0), ("OD", 1, 1, 0), ("C", 1, 2, 0),
+    ("OD", 1, 2, 0), ("Z", 0, 2, 3, 1), ("Z", 0, 2, 3, 0), ("SC", 3, 1), ("C", 1, 2, 1),
+    ("OD", 1, 2, 1), ("C", 1, 1, 1), ("OD", 1, 1, 1), ("SC", 3, 0), ("SR", 3, 1), ("C", 0, 3, 1),
+    ("SC", 0, 2), ("OL1", 0, 1, 1), ("SR", 3, 0), ("C", 0, 3, 0), ("C", 1, 3, 1), ("OL1", 0, 0, 0),
+    ("OL1", 0, 0, 1), ("OL1", 1, 0, 1), ("OL1", 0, 1, 0), ("SR", 0, 2), ("C", 1, 3, 0),
+    ("OL1", 1, 1, 0), ("C", 1, 0, 2), ("OL1", 1, 1, 1), ("OL1", 1, 0, 0), ("OL2", 0, 0, 0),
+    ("OL2", 0, 1, 1), ("OL2", 0, 0, 1), ("OL2", 0, 1, 0), ("OL2", 1, 0, 1), ("OL2", 1, 1, 0),
+    ("OL2", 1, 0, 0), ("OL2", 1, 1, 1), ("C", 0, 0, 2),
 )
 
 
@@ -64,6 +65,7 @@
     x_to = [(row, yh * 4 + xs[1]), (row, yh * 4 + xs[3])]
     y_to = [(row, ys[1] * 4 + x), (row, ys[3] * 4 + x)]
     z_to = [(zs[1] * 4 + low, col), (zs[7] * 4 + low, col)]
+    z_skip = [(zs[2] * 4 + low, col), (zs[6] * 4 + low, col)]
     pair = (z * 4 + (1 - yl) * 2 + core, col)
     twin = (row + 1 - 2 * core, col)
     s_to = {
@@ -124,17 +126,19 @@
             ).wait_recv()
 
     def Z(o, u, s, d):
-        if s:
-            need("Z", o, u, s - 1, d)
+        skip = (o, u) in SKIPS
+        back = (0, 0, 2, 2)[s] if skip else s
+        if back:
+            need("Z", o, u, back - 1, d)
         else:
             for c in halves(u):
                 s_came(o, c)
                 if o == 0:
                     here(("S", c))
-        part = sbuf.at[block[o], slice(0, 2) if u == 2 else u, core, zs[(-s, s)[d]]]
+        part = sbuf.at[block[o], slice(0, 2) if u == 2 else u, core, zs[(-back, back)[d]]]
         if s == 3:
             part = part.at[:, d] if u == 2 else part.at[d]
-        send(("Z", o, u, s, d), part, part, z_to[d])
+        send(("Z", o, u, s, d), part, part, (z_skip if skip and s in (1, 3) else z_to)[d])
 
     def SC(o, u):
         for d in range(2):
@@ -249,7 +253,7 @@
         send(("OL2", p, d, u), orel.at[p, d, :, cols(u)], dst, y_to[d])
 
     barrier = pltpu.get_barrier_semaphore()
-    peers = (*x_to, *z_to, pair, twin, *s_to.values())
+    peers = (*x_to, *z_to, *(z_skip if SKIPS else ()), pair, twin, *s_to.values())
     for device in peers:
         pl.semaphore_signal(barrier, inc=1, device_id=device, device_id_type=MESH)
     for c in range(2):

time: 69.6 us -> 69 us (level)
  no operation moved by 1% of the time
where the time goes in v4:
time: 69 us; the launch traced here: 68.1 us
  Pallas kernels  67.1 us (97%)
  local copies, waits for them, and re-layouts  0.97 us (1%)
    pallas_call x1, Pallas kernels, body(): pl.pallas_call(kernel, out_shape=jax.ShapeDtypeStruct((4, PASSES, H, 256)...  67.1 us

profile of v4, /device:TPU:1, one launch (start us, length us, event | category | flops | bytes accessed | tf_op | source)
XLA Modules:
  0.0 68.1 jit_solution(3272266785702342593)
XLA Ops:
  0.0 67.1 %shard_map.64 = bf16[4,2,256,256]{3,2,1,0:T(8,128)(2,1)S(1)} custom-call(bf16[4,2,256,128]{3,2,1,0:T(8,128)(2,1)} %bitcast.6, bf16[64,256]{1,0:T(8,128)(2,1)} %s_ref.1, bf16[2,2,4,256,128]{4,3,2,1,0:T(8,128)(2,1)} %bitcast.5, s32[16,512]{1,0:T(8,128)} %bitcast.7, s32[16,32]{1,0:T(8,128)} %sp_ref.1, s32[32,512]{1,0:T(8,128)} %tp_ref.1), custom_call_target="tpu_custom_call" | custom-call | tf_op jit(solution)/shard_map/pallas_call | solution.py:287
  67.1 1.0 %copy.8 = bf16[2048,256]{1,0:T(8,128)(2,1)} copy(bf16[2048,256]{1,0:T(8,128)(2,1)S(1)} %bitcast.4) | data formatting | bytes 2097152

commit v5 on v4

--- a/solution.py
+++ b/solution.py
@@ -10,44 +10,44 @@
 PASSES = 2
 H = 512 // PASSES
 UNITS = {0: (2,), 1: (0, 1), 2: (0, 1), 3: (0, 1)}
-SKIPS = ((1, 0), (2, 0))
+SKIPS = ((1, 0), (1, 1), (2, 0), (2, 1))
 ORDER = (
-    ("SU", 1, 0, 0), ("SU", 2, 1, 0), ("SU", 0, 0, 1), ("TD", 0, 0), ("SU", 1, 1, 0), ("RL1", 0, 1),
-    ("RX", 0, 0, 1), ("SU", 2, 0, 1), ("SU", 1, 0, 1), ("SU", 2, 0, 0), ("TL1", 0, 1),
-    ("SU", 2, 1, 1), ("SU", 1, 1, 1), ("RY", 0, 1), ("RX", 0, 1, 0), ("TD", 0, 1), ("TL1", 0, 0),
-    ("RL1", 0, 0), ("SU", 0, 0, 0), ("RY", 0, 0), ("Z", 1, 0, 1, 1), ("Z", 1, 0, 1, 0),
-    ("SU", 3, 0, 1), ("Z", 2, 0, 1, 0), ("Z", 2, 0, 1, 1), ("RL2", 0, 1), ("RF", 0, 1, 0),
-    ("RL1", 1, 1), ("Z", 2, 1, 0, 0), ("Z", 1, 0, 0, 0), ("RX", 0, 1, 1), ("Z", 2, 1, 0, 1),
-    ("RX", 0, 0, 0), ("Z", 1, 1, 0, 1), ("RL2", 0, 0), ("TL2", 0, 0), ("Z", 2, 0, 0, 1),
-    ("RF", 0, 0, 1), ("RL1", 1, 0), ("SU", 3, 1, 1), ("TL2", 0, 1), ("Z", 1, 1, 0, 0),
-    ("Z", 1, 0, 0, 1), ("SU", 3, 1, 0), ("Z", 1, 0, 3, 0), ("SU", 3, 0, 0), ("Z", 1, 0, 3, 1),
-    ("RX", 2, 0, 1), ("Z", 1, 0, 2, 0), ("RX", 1, 0, 0), ("RY", 1, 1), ("RX", 2, 0, 0),
-    ("RY", 1, 0), ("Z", 1, 0, 2, 1), ("Z", 2, 1, 1, 0), ("Z", 2, 0, 3, 0), ("Z", 2, 1, 1, 1),
-    ("RX", 1, 0, 1), ("Z", 1, 1, 1, 1), ("Z", 2, 0, 3, 1), ("Z", 1, 1, 1, 0), ("RH", 1, 0, 1),
-    ("Z", 2, 0, 2, 0), ("TL1", 1, 1), ("Z", 2, 0, 0, 0), ("RH", 0, 0, 0), ("Z", 2, 0, 2, 1),
-    ("RH", 0, 0, 1), ("RL2", 1, 1), ("RH", 1, 0, 0), ("Z", 3, 1, 0, 1), ("Z", 3, 1, 0, 0),
-    ("SC", 1, 0), ("RF", 0, 0, 0), ("RF", 1, 0, 0), ("RL2", 1, 0), ("RF", 2, 0, 1),
-    ("Z", 2, 1, 2, 1), ("Z", 2, 1, 2, 0), ("Z", 1, 1, 2, 1), ("Z", 3, 0, 0, 0), ("Z", 3, 0, 0, 1),
-    ("Z", 1, 1, 2, 0), ("Z", 0, 2, 0, 0), ("RF", 1, 0, 1), ("RF", 2, 0, 0), ("RF", 3, 0, 0),
-    ("RF", 3, 0, 1), ("Z", 0, 2, 0, 1), ("SR", 1, 0), ("SC", 2, 0), ("RX", 2, 1, 0),
-    ("RX", 1, 1, 0), ("RX", 2, 1, 1), ("Z", 2, 1, 3, 1), ("Z", 2, 1, 3, 0), ("Z", 3, 1, 1, 1),
-    ("RX", 1, 1, 1), ("Z", 3, 1, 1, 0), ("Z", 1, 1, 3, 1), ("Z", 3, 0, 1, 1), ("RH", 1, 1, 1),
-    ("Z", 1, 1, 3, 0), ("SR", 2, 0), ("Z", 3, 0, 1, 0), ("RH", 0, 1, 0), ("RR", 0),
-    ("Z", 0, 2, 1, 1), ("Z", 0, 2, 1, 0), ("TL1", 1, 0), ("RF", 0, 1, 1), ("SC", 2, 1),
-    ("C", 0, 2, 0), ("RF", 2, 1, 0), ("RF", 2, 1, 1), ("Z", 3, 1, 2, 0), ("C", 0, 1, 0),
-    ("Z", 3, 1, 2, 1), ("SC", 1, 1), ("RH", 0, 1, 1), ("RF", 1, 1, 0), ("RF", 1, 1, 1),
-    ("Z", 3, 0, 2, 1), ("Z", 3, 0, 2, 0), ("OD", 0, 2, 0), ("OD", 0, 1, 0), ("RF", 3, 1, 0),
-    ("RF", 3, 1, 1), ("RH", 1, 1, 0), ("SR", 2, 1), ("C", 0, 2, 1), ("Z", 0, 2, 2, 1),
-    ("Z", 0, 2, 2, 0), ("OD", 0, 2, 1), ("TD", 1, 0), ("TD", 1, 1), ("SR", 1, 1), ("Z", 3, 1, 3, 0),
-    ("TL2", 1, 0), ("C", 0, 1, 1), ("Z", 3, 1, 3, 1), ("OD", 0, 1, 1), ("Z", 3, 0, 3, 0),
-    ("TL2", 1, 1), ("Z", 3, 0, 3, 1), ("RR", 1), ("C", 1, 1, 0), ("OD", 1, 1, 0), ("C", 1, 2, 0),
-    ("OD", 1, 2, 0), ("Z", 0, 2, 3, 1), ("Z", 0, 2, 3, 0), ("SC", 3, 1), ("C", 1, 2, 1),
-    ("OD", 1, 2, 1), ("C", 1, 1, 1), ("OD", 1, 1, 1), ("SC", 3, 0), ("SR", 3, 1), ("C", 0, 3, 1),
-    ("SC", 0, 2), ("OL1", 0, 1, 1), ("SR", 3, 0), ("C", 0, 3, 0), ("C", 1, 3, 1), ("OL1", 0, 0, 0),
-    ("OL1", 0, 0, 1), ("OL1", 1, 0, 1), ("OL1", 0, 1, 0), ("SR", 0, 2), ("C", 1, 3, 0),
-    ("OL1", 1, 1, 0), ("C", 1, 0, 2), ("OL1", 1, 1, 1), ("OL1", 1, 0, 0), ("OL2", 0, 0, 0),
-    ("OL2", 0, 1, 1), ("OL2", 0, 0, 1), ("OL2", 0, 1, 0), ("OL2", 1, 0, 1), ("OL2", 1, 1, 0),
-    ("OL2", 1, 0, 0), ("OL2", 1, 1, 1), ("C", 0, 0, 2),
+    ("SU", 1, 0, 0), ("TL1", 0, 0), ("SU", 2, 1, 0), ("SU", 2, 0, 0), ("RX", 0, 1, 0),
+    ("RL1", 0, 0), ("SU", 1, 1, 0), ("SU", 2, 0, 1), ("TL1", 0, 1), ("RL1", 0, 1), ("SU", 2, 1, 1),
+    ("RX", 0, 0, 1), ("RY", 0, 1), ("TD", 0, 0), ("TD", 0, 1), ("TL1", 1, 1), ("RY", 0, 0),
+    ("SU", 1, 0, 1), ("Z", 1, 0, 1, 0), ("Z", 1, 0, 1, 1), ("Z", 2, 0, 1, 0), ("TD", 1, 0),
+    ("RX", 0, 1, 1), ("RX", 0, 0, 0), ("SU", 3, 0, 0), ("SU", 1, 1, 1), ("Z", 1, 0, 0, 1),
+    ("Z", 1, 0, 0, 0), ("RL2", 0, 1), ("SU", 0, 0, 0), ("SU", 3, 1, 0), ("Z", 2, 0, 1, 1),
+    ("Z", 2, 0, 0, 0), ("RL2", 0, 0), ("Z", 2, 1, 1, 0), ("RL1", 1, 0), ("Z", 2, 1, 0, 1),
+    ("Z", 2, 0, 0, 1), ("RL1", 1, 1), ("RF", 0, 0, 1), ("RX", 2, 0, 1), ("SU", 3, 0, 1),
+    ("SU", 3, 1, 1), ("RY", 1, 0), ("RX", 2, 0, 0), ("Z", 1, 0, 3, 1), ("RY", 1, 1),
+    ("Z", 1, 0, 3, 0), ("Z", 1, 0, 2, 1), ("RX", 1, 0, 0), ("Z", 1, 0, 2, 0), ("RX", 1, 0, 1),
+    ("Z", 1, 1, 1, 1), ("Z", 1, 1, 1, 0), ("RH", 1, 0, 0), ("RF", 0, 0, 0), ("Z", 1, 1, 0, 1),
+    ("RH", 1, 0, 1), ("RF", 0, 1, 1), ("Z", 3, 0, 0, 0), ("RH", 0, 0, 1), ("RH", 0, 0, 0),
+    ("SU", 0, 0, 1), ("Z", 2, 1, 1, 1), ("TL2", 0, 0), ("RF", 2, 0, 1), ("TL2", 0, 1),
+    ("Z", 2, 0, 2, 0), ("Z", 3, 0, 0, 1), ("Z", 2, 0, 3, 1), ("Z", 2, 0, 3, 0), ("Z", 2, 1, 2, 0),
+    ("RF", 2, 0, 0), ("RL2", 1, 1), ("Z", 2, 0, 2, 1), ("RL2", 1, 0), ("SC", 1, 0), ("RF", 1, 0, 0),
+    ("Z", 3, 1, 0, 0), ("Z", 3, 1, 0, 1), ("RF", 3, 0, 1), ("Z", 1, 1, 3, 1), ("RF", 1, 0, 1),
+    ("Z", 1, 1, 0, 0), ("Z", 1, 1, 2, 1), ("Z", 1, 1, 3, 0), ("Z", 1, 1, 2, 0), ("Z", 2, 1, 3, 0),
+    ("RF", 3, 0, 0), ("SR", 1, 0), ("Z", 3, 0, 1, 0), ("RX", 2, 1, 1), ("RX", 2, 1, 0),
+    ("Z", 3, 0, 1, 1), ("Z", 2, 1, 3, 1), ("RX", 1, 1, 0), ("Z", 2, 1, 0, 0), ("RX", 1, 1, 1),
+    ("Z", 2, 1, 2, 1), ("Z", 3, 1, 1, 0), ("SC", 2, 0), ("RH", 0, 1, 0), ("Z", 0, 2, 0, 0),
+    ("RH", 1, 1, 0), ("Z", 3, 1, 1, 1), ("Z", 0, 2, 0, 1), ("RH", 1, 1, 1), ("RR", 0),
+    ("TL2", 1, 1), ("C", 0, 1, 0), ("SC", 1, 1), ("RH", 0, 1, 1), ("SR", 2, 0), ("Z", 3, 0, 2, 1),
+    ("RF", 0, 1, 0), ("Z", 3, 0, 2, 0), ("RF", 2, 1, 1), ("C", 0, 2, 0), ("RF", 2, 1, 0),
+    ("SC", 2, 1), ("RF", 1, 1, 0), ("OD", 0, 2, 0), ("RF", 1, 1, 1), ("OD", 0, 1, 0),
+    ("Z", 3, 1, 2, 0), ("SR", 1, 1), ("Z", 3, 1, 2, 1), ("RF", 3, 1, 0), ("RF", 3, 1, 1),
+    ("TL1", 1, 0), ("TD", 1, 1), ("C", 0, 1, 1), ("Z", 3, 0, 3, 0), ("SR", 2, 1), ("Z", 3, 0, 3, 1),
+    ("C", 0, 2, 1), ("OD", 0, 1, 1), ("OD", 0, 2, 1), ("Z", 0, 2, 1, 0), ("Z", 0, 2, 1, 1),
+    ("Z", 3, 1, 3, 0), ("Z", 3, 1, 3, 1), ("RR", 1), ("C", 1, 2, 0), ("C", 1, 1, 0),
+    ("OD", 1, 2, 0), ("OD", 1, 1, 0), ("TL2", 1, 0), ("SC", 3, 0), ("C", 1, 2, 1),
+    ("Z", 0, 2, 2, 0), ("Z", 0, 2, 2, 1), ("OD", 1, 2, 1), ("SC", 3, 1), ("C", 1, 1, 1),
+    ("OD", 1, 1, 1), ("SR", 3, 0), ("C", 1, 3, 0), ("SR", 3, 1), ("OL1", 1, 1, 0), ("C", 1, 3, 1),
+    ("OL1", 1, 0, 0), ("OL1", 1, 1, 1), ("Z", 0, 2, 3, 1), ("C", 0, 3, 0), ("OL1", 0, 1, 0),
+    ("OL1", 0, 0, 0), ("C", 0, 3, 1), ("Z", 0, 2, 3, 0), ("OL1", 1, 0, 1), ("OL1", 0, 1, 1),
+    ("OL1", 0, 0, 1), ("SC", 0, 2), ("OL2", 1, 1, 0), ("OL2", 1, 0, 0), ("OL2", 0, 0, 0),
+    ("OL2", 1, 1, 1), ("OL2", 0, 1, 0), ("OL2", 1, 0, 1), ("SR", 0, 2), ("OL2", 0, 0, 1),
+    ("OL2", 0, 1, 1), ("C", 1, 0, 2), ("C", 0, 0, 2),
 )
 
 

time: 69 us -> 69.5 us (level); the launches traced: 68.1 us -> 69.4 us
  Pallas kernels: 67.1 us -> 68.4 us
    pallas_call x1, Pallas kernels: 67.1 us -> 68.4 us  [body(): pl.pallas_call(kernel, out_shape=jax.ShapeDtypeStruct((4, PASSES, H, 256)...]
where the time goes in v5:
time: 69.5 us; the launch traced here: 69.4 us
  Pallas kernels  68.4 us (98%)
  local copies, waits for them, and re-layouts  0.97 us (1%)
    pallas_call x1, Pallas kernels, body(): pl.pallas_call(kernel, out_shape=jax.ShapeDtypeStruct((4, PASSES, H, 256)...  68.4 us

profile of v5, /device:TPU:1, one launch (start us, length us, event | category | flops | bytes accessed | tf_op | source)
XLA Modules:
  0.0 69.4 jit_solution(13621665540068275061)
XLA Ops:
  0.0 68.4 %shard_map.64 = bf16[4,2,256,256]{3,2,1,0:T(8,128)(2,1)S(1)} custom-call(bf16[4,2,256,128]{3,2,1,0:T(8,128)(2,1)} %bitcast.6, bf16[64,256]{1,0:T(8,128)(2,1)} %s_ref.1, bf16[2,2,4,256,128]{4,3,2,1,0:T(8,128)(2,1)} %bitcast.5, s32[16,512]{1,0:T(8,128)} %bitcast.7, s32[16,32]{1,0:T(8,128)} %sp_ref.1, s32[32,512]{1,0:T(8,128)} %tp_ref.1), custom_call_target="tpu_custom_call" | custom-call | tf_op jit(solution)/shard_map/pallas_call | solution.py:287
  68.4 1.0 %copy.8 = bf16[2048,256]{1,0:T(8,128)(2,1)} copy(bf16[2048,256]{1,0:T(8,128)(2,1)S(1)} %bitcast.4) | data formatting | bytes 2097152
